TPU v7x, 512 devices: a whole 4x4x16 slice. The times are simulated.
512 devices in a mesh: inst: 16 (over z), span: 8 (over x, y_lo), chord: 4 (over y_hi, core).
Axes of the slice: x: 4, y: 4 (y_hi: 2, y_lo: 2; y = y_hi * 2 + y_lo), z: 16, core: 2. Of those that a mesh axis runs over, the one named last changes fastest.
Arguments:
- adj_source: float32 [16, 32, 32, 1920], P('inst', 'span', 'chord'), may hold values from -6 to 6
- adj_start: float32 [16, 32, 32, 1920], P('inst', 'span', 'chord'), may hold values from -4 to 4
- tiles: bfloat16 [16, 32, 32, 4, 6, 1920], P('inst', 'span', 'chord'), may hold values from -1.25 to 1.25
- tile_cols: int32 [32, 32, 4], P('span', 'chord'), may hold values from 0 to 8, as said below
- inverse_diag: bfloat16 [16, 32, 32, 6, 1920], P('inst', 'span', 'chord'), as said below
- face_src: int32 [2, 8192], P(None, ('span', 'chord')), may hold values from 0 to 10239, as said below
- face_dst: int32 [2, 8192], P(None, ('span', 'chord')), may hold values from 0 to 10239, as said below
- lag_coef: bfloat16 [16, 72, 8192], P('inst', None, ('span', 'chord')), may hold values from -2.5 to 2.5
Outputs:
- adjoint: float32 [16, 32, 32, 1920], P('inst', 'span', 'chord')
- residual: float32 [16, 32, 32, 1920], P('inst', 'span', 'chord')
Inputs may be any that keep to these rules, and one draw needn't show every extreme that they name: `tile_cols`: each block row names code 4 (its own block) once and three distinct other codes; code 3 a + b means the block a - 1 spanwise and b - 1 chordwise away. `face_src`: for each side, the 256 entries of one span and chord group are distinct cell numbers of that group. `face_dst`: for each side, the 256 entries of one span and chord group are distinct cell numbers of that group. `inverse_diag`: diagonal entries of each 6 x 6 block lie in 0.4 to 1.6, off-diagonal entries in -0.35 to 0.35.
All inputs are finite; a program needn't handle non-finite values.
Results may differ from a plain program's by a relative error of at most 0.0003.
Values sent between devices are 32-bit elements; how exact they have to be, the bound alone decides.
No kernel may reach another device: no remote copies, remote signals or barrier semaphores. Data moves between devices by JAX's collectives and lax.ppermute only.
A program may use at most 64 MiB of HBM per device.

v0:
```python
import math

import jax
import jax.numpy as jnp
from jax import lax
from jax.experimental import pallas as pl
from jax.experimental.pallas import tpu as pltpu
from jax.sharding import PartitionSpec as P

NV = 6
BLK = 320
SB = 4
CB = 8
K = 4
PF = 256
SWEEPS = 2
NT = 16
LAG = 4
WIDTH = NV * BLK
LANES = 128
STRIPS = WIDTH // LANES
SHARE = 32
FACE_ROW = SB * STRIPS * 8

rotor_rate = 0.25
spectral_viscosity = 0.03


def spectral_coefficients():
    values = []
    for offset in range(NT):
        parity = 1.0 if offset % 2 == 0 else -1.0
        if offset == 0:
            first, second = 0.0, -(NT * NT + 2) / 12.0
        else:
            angle = math.pi * offset / NT
            first = 0.5 * parity * math.cos(angle) / math.sin(angle)
            second = -0.5 * parity / math.sin(angle) ** 2
        values.append(rotor_rate * first - spectral_viscosity * second)
    return values


def split_cells(cells):
    block = lax.shift_right_logical(cells * 6554, 21)
    return block, cells - block * BLK


def three_parts(value):
    high = value.astype(jnp.bfloat16)
    rest = value - high.astype(jnp.float32)
    middle = rest.astype(jnp.bfloat16)
    low = (rest - middle.astype(jnp.float32)).astype(jnp.bfloat16)
    return high, middle, low


def one_hot(size, row):
    hit = lax.broadcasted_iota(jnp.int32, (size, row.shape[1]), 0) == row
    return jnp.where(hit, 1.0, 0.0).astype(jnp.bfloat16)


def emit_exchange(state_ref, src_ref, send_ref):
    for p in range(SB):
        for strip in range(STRIPS):
            row = (p * STRIPS + strip) * 8
            send_ref[row : row + 8, :] = state_ref[p, :, strip * LANES : (strip + 1) * LANES]
    flat = [
        jnp.concatenate([state_ref[p, :, w * BLK : (w + 1) * BLK] for p in range(SB)], axis=0)
        for w in range(NV)
    ]
    rows = SB * CB
    parts = [three_parts(value) for value in flat]
    stacked = jnp.concatenate([parts[w][n] for n in range(3) for w in range(NV)], axis=0)
    for side in range(2):
        block, cell = split_cells(src_ref[side : side + 1, :])
        picked = jnp.dot(stacked, one_hot(BLK, cell), preferred_element_type=jnp.float32)
        count = NV * rows
        picked = picked[:count] + (picked[count : 2 * count] + picked[2 * count :])
        mine = lax.broadcasted_iota(jnp.int32, (rows, PF), 0) == block
        pack = jnp.concatenate(
            [
                jnp.sum(jnp.where(mine, picked[w * rows : (w + 1) * rows], 0.0), axis=0, keepdims=True)
                for w in range(NV)
            ]
            + [jnp.zeros((8 - NV, PF), jnp.float32)],
            axis=0,
        )
        for half in range(2):
            row = FACE_ROW + side * 16 + half * 8
            send_ref[row : row + 8, :] = pack[:, half * LANES : (half + 1) * LANES]


def emit_edges(state_ref, low_ref, high_ref):
    for p in range(SB):
        low_ref[p : p + 1, :] = state_ref[p, CB - 1 : CB, :]
        high_ref[p : p + 1, :] = state_ref[p, 0:1, :]


def start_kernel(state_ref, src_ref, send_ref):
    emit_exchange(state_ref, src_ref, send_ref)


def spectral_kernel(who_ref, in_ref, out_ref):
    coef = spectral_coefficients()
    half = NT // 2

    @pl.when(who_ref[0] != NT - 1)
    def _():
        for group in range(SHARE // 8):
            rows = slice(group * 8, group * 8 + 8)
            sums = [in_ref[s, rows, :] + in_ref[s + half, rows, :] for s in range(half)]
            gaps = [in_ref[s, rows, :] - in_ref[s + half, rows, :] for s in range(half)]
            for t in range(half):
                even = odd = None
                for s in range(half):
                    near, far = coef[(s - t) % NT], coef[(s - t + half) % NT]
                    one = sums[s] * jnp.float32(0.5 * (near + far))
                    two = gaps[s] * jnp.float32(0.5 * (near - far))
                    even = one if even is None else even + one
                    odd = two if odd is None else odd + two
                out_ref[t, rows, :] = even + odd
                out_ref[t + half, rows, :] = even - odd

    @pl.when(who_ref[0] == NT - 1)
    def _():
        for t in range(NT):
            out_ref[t, 0:16, :] = in_ref[(t - LAG) % NT, 0:16, :]
            out_ref[t, 16:32, :] = in_ref[(t + LAG) % NT, 16:32, :]


def fold(product):
    pair = 2 * BLK
    total = product[:, :pair] + product[:, pair : 2 * pair] + product[:, 2 * pair :]
    return total[:, :BLK] + total[:, BLK:]


def put(ref, row, count, value):
    ref[0, pl.ds(row, count), :] = value[:, :LANES]
    ref[1, pl.ds(row, count), :] = value[:, LANES : 2 * LANES]
    ref[2, pl.ds(row, count), 0 : BLK - 2 * LANES] = value[:, 2 * LANES :]


def take(ref, row):
    parts = [ref[n, pl.ds(row, CB, stride=8), :] for n in range(3)]
    return jnp.concatenate(parts, axis=1)[:, :BLK]


def tile_kernel(
    cols_ref, tiles_ref, state_ref, left_ref, right_ref, below_ref, above_ref, source_ref, out_ref, wide, term
):
    p = pl.program_id(0)

    @pl.when(p == 0)
    def _():
        wide[0:10, :] = below_ref[...]
        wide[(SB + 1) * 16 : (SB + 1) * 16 + 10, :] = above_ref[...]
        for row in range(SB):
            base = (row + 1) * 16
            wide[base : base + 8, :] = state_ref[row]
            wide[base + 8 : base + 9, :] = left_ref[row : row + 1, :]
            wide[base + 9 : base + 10, :] = right_ref[row : row + 1, :]

    def block(q, carry):
        total = None
        for k in range(K):
            code = cols_ref[p, q, k]
            a = lax.div(code, 3)
            side = q + code - 3 * a - 1
            column = jnp.where(side < 0, CB, jnp.where(side == CB, CB + 1, side))
            row = (p + a) * 16 + column
            product = tiles_ref[0, q, k].astype(jnp.float32) * wide[pl.ds(row, 1), :]
            total = product if total is None else total + product
        put(term, pl.multiple_of(q * 8, 8), NV, fold(total))
        return carry

    lax.fori_loop(0, CB, block, 0)
    for v in range(NV):
        lanes = slice(v * BLK, (v + 1) * BLK)
        out_ref[0, :, lanes] = source_ref[0, :, lanes] - take(term, v)


def finish(base_ref, spectral_ref, state_ref, inverse_ref, coef_ref, dst_ref, residual_ref, next_ref, lagged, term):
    coef = coef_ref[...].astype(jnp.float32)
    spread, cells = [], []
    for side in range(2):
        row = FACE_ROW + side * 16
        pack = jnp.concatenate([spectral_ref[row : row + NV, :], spectral_ref[row + 8 : row + 8 + NV, :]], axis=1)
        contrib = []
        for v in range(NV):
            at = (side * NV + v) * NV
            contrib.append(jnp.sum(coef[at : at + NV] * pack, axis=0, keepdims=True))
        contrib = jnp.concatenate(contrib + [jnp.zeros((8 - NV, PF), jnp.float32)], axis=0)
        block, cell = split_cells(dst_ref[side : side + 1, :])
        spread.append(
            jnp.concatenate([jnp.where(block == b, contrib, 0.0) for b in range(SB * CB)], axis=0)
        )
        cells.append(one_hot(BLK, cell))
    stacked = jnp.concatenate(three_parts(jnp.concatenate(spread, axis=1)), axis=0)
    placed = lax.dot_general(
        stacked,
        jnp.concatenate(cells, axis=1),
        (((1,), (1,)), ((), ())),
        preferred_element_type=jnp.float32,
    )
    count = SB * CB * 8
    put(lagged, 0, count, placed[:count] + (placed[count : 2 * count] + placed[2 * count :]))
    for p in range(SB):
        first = p * STRIPS * 8
        spectral = jnp.concatenate(
            [spectral_ref[first + 8 * n : first + 8 * n + 8, :] for n in range(STRIPS)], axis=1
        )
        residual_ref[p] = base_ref[p] - spectral
        for v in range(NV):
            lanes = slice(v * BLK, (v + 1) * BLK)
            residual_ref[p, :, lanes] = (
                residual_ref[p, :, lanes] - take(lagged, p * CB * 8 + v)
            )

        def block(q, carry):
            product = inverse_ref[p, q].astype(jnp.float32) * residual_ref[p, pl.ds(q, 1), :]
            put(term, pl.multiple_of(q * 8, 8), NV, fold(product))
            return carry

        lax.fori_loop(0, CB, block, 0, unroll=True)
        for v in range(NV):
            lanes = slice(v * BLK, (v + 1) * BLK)
            next_ref[p, :, lanes] = state_ref[p, :, lanes] + take(term, v)


def middle_kernel(
    base_ref, spectral_ref, state_ref, inverse_ref, coef_ref, dst_ref, src_ref, next_ref, send_ref, low_ref, high_ref, residual_ref, lagged, term
):
    finish(base_ref, spectral_ref, state_ref, inverse_ref, coef_ref, dst_ref, residual_ref, next_ref, lagged, term)
    emit_exchange(next_ref, src_ref, send_ref)
    emit_edges(next_ref, low_ref, high_ref)


def last_kernel(
    base_ref, spectral_ref, state_ref, inverse_ref, coef_ref, dst_ref, next_ref, residual_ref, lagged, term
):
    finish(base_ref, spectral_ref, state_ref, inverse_ref, coef_ref, dst_ref, residual_ref, next_ref, lagged, term)


def f32(*shape):
    return jax.ShapeDtypeStruct(shape, jnp.float32)


STATE = f32(SB, CB, WIDTH)
EDGE = f32(SB, WIDTH)
SEND = f32(NT * SHARE, LANES)
FINISH_SCRATCH = [pltpu.VMEM((3, SB * CB * 8, LANES), jnp.float32), pltpu.VMEM((3, CB * 8, LANES), jnp.float32)]
ROOM = pltpu.CompilerParams(vmem_limit_bytes=32 << 20)


def start_call(state, src):
    return pl.pallas_call(start_kernel, out_shape=SEND, compiler_params=ROOM)(state, src)


def spectral_call(who, received):
    return pl.pallas_call(
        spectral_kernel,
        out_shape=f32(NT, SHARE, LANES),
        in_specs=[pl.BlockSpec(memory_space=pltpu.SMEM), pl.BlockSpec(memory_space=pltpu.VMEM)],
        compiler_params=ROOM,
    )(who, received)


def tile_call(cols, tiles, state, left, right, below, above, source):
    whole = lambda array: pl.BlockSpec(array.shape, lambda p: (0,) * array.ndim)
    return pl.pallas_call(
        tile_kernel,
        out_shape=STATE,
        grid=(SB,),
        in_specs=[
            pl.BlockSpec(memory_space=pltpu.SMEM),
            pl.BlockSpec((1, CB, K, NV, WIDTH), lambda p: (p, 0, 0, 0, 0)),
            whole(state),
            whole(left),
            whole(right),
            whole(below),
            whole(above),
            pl.BlockSpec((1, CB, WIDTH), lambda p: (p, 0, 0)),
        ],
        out_specs=pl.BlockSpec((1, CB, WIDTH), lambda p: (p, 0, 0)),
        scratch_shapes=[
            pltpu.VMEM(((SB + 2) * 16, WIDTH), jnp.float32),
            pltpu.VMEM((3, CB * 8, LANES), jnp.float32),
        ],
        compiler_params=ROOM,
    )(cols, tiles, state, left, right, below, above, source)


def middle_call(base, spectral, state, inverse, coef, dst, src):
    return pl.pallas_call(
        middle_kernel,
        out_shape=(STATE, SEND, EDGE, EDGE),
        scratch_shapes=[pltpu.VMEM((SB, CB, WIDTH), jnp.float32)] + FINISH_SCRATCH,
        compiler_params=ROOM,
    )(base, spectral, state, inverse, coef, dst, src)


def last_call(base, spectral, state, inverse, coef, dst):
    return pl.pallas_call(
        last_kernel,
        out_shape=(STATE, STATE),
        scratch_shapes=FINISH_SCRATCH,
        compiler_params=ROOM,
    )(base, spectral, state, inverse, coef, dst)


def exchange(array):
    return lax.all_to_all(array, "inst", 0, 0, tiled=True)


def halos(state, low_edge, high_edge):
    n = lax.axis_size("chord")
    left = lax.ppermute(low_edge, "chord", [(i, (i + 1) % n) for i in range(n)])
    right = lax.ppermute(high_edge, "chord", [(i, (i - 1) % n) for i in range(n)])
    n = lax.axis_size("span")
    last = jnp.concatenate([state[SB - 1], left[SB - 1 :], right[SB - 1 :]], axis=0)
    first = jnp.concatenate([state[0], left[:1], right[:1]], axis=0)
    below = lax.ppermute(last, "span", [(i, i + 1) for i in range(n - 1)])
    above = lax.ppermute(first, "span", [(i + 1, i) for i in range(n - 1)])
    return left, right, below, above


def per_device(adj_source, adj_start, tiles, tile_cols, inverse_diag, face_src, face_dst, lag_coef):
    source, state = adj_source[0], adj_start[0]
    tiles, inverse, coef = tiles[0], inverse_diag[0], lag_coef[0]
    who = lax.axis_index("inst").astype(jnp.int32)[None]
    send = start_call(state, face_src)
    low_edge, high_edge = state[:, CB - 1], state[:, 0]
    for sweep in range(SWEEPS):
        received = exchange(send.reshape(NT, SHARE, LANES))
        left, right, below, above = halos(state, low_edge, high_edge)
        spectral = exchange(spectral_call(who, received)).reshape(NT * SHARE, LANES)
        base = tile_call(tile_cols, tiles, state, left, right, below, above, source)
        if sweep < SWEEPS - 1:
            state, send, low_edge, high_edge = middle_call(
                base, spectral, state, inverse, coef, face_dst, face_src
            )
        else:
            state, residual = last_call(base, spectral, state, inverse, coef, face_dst)
    return state[None], residual[None]


def solution(mesh):
    return jax.shard_map(
        per_device,
        mesh=mesh,
        in_specs=(
            P("inst", "span", "chord", None),
            P("inst", "span", "chord", None),
            P("inst", "span", "chord", None, None, None),
            P("span", "chord", None),
            P("inst", "span", "chord", None, None),
            P(None, ("span", "chord")),
            P(None, ("span", "chord")),
            P("inst", None, ("span", "chord")),
        ),
        out_specs=(P("inst", "span", "chord", None), P("inst", "span", "chord", None)),
        check_vma=False,
    )
```

profile of v0, /device:TPU:58, one launch (start us, length us, event | category | flops | bytes accessed | tf_op | source)
XLA Modules:
  0.0 119.7 jit_solution(3891205941938879548)
XLA Ops:
  0.6 0.0 copy-start.2
  0.6 0.9 copy-done.2
  1.6 0.0 copy-start.6
  1.6 0.7 copy-done.6
  2.3 1.2 %shard_map.96 = f32[512,128]{1,0:T(8,128)} custom-call(f32[4,8,1920]{2,1,0:T(8,128)S(1)} %bitcast.34, s32[2,256]{1,0:T(2,128)S(1)} %copy-done.6), custom_call_target="tpu_custom_call" | custom-call | tf_op jit(solution)/shard_map/pallas_call | solution.py:255
  3.5 15.2 %all-to-all-start = ((f32[16,32,128]{2,1,0:T(8,128)}), f32[16,32,128]{2,1,0:T(8,128)S(1)}, u32[]{:S(2)}, u32[]{:S(2)}) async-start(f32[16,32,128]{2,1,0:T(8,128)} %bitcast.6), calls=%async_computation | async-start | bytes 524288 | tf_op jit(solution)/shard_map/all_to_all | solution.py:311
  18.7 1.9 %collective-permute-start = (f32[4,1920]{1,0:T(4,128)S(1)}, f32[4,1920]{1,0:T(4,128)S(1)}, u32[]{:S(2)}, u32[]{:S(2)}) collective-permute-start(f32[4,1920]{1,0:T(4,128)S(1)} %bitcast.44), channel_id=1, source_target_pairs={{0,1},{1,2},{2,3},{3,0},{4,5},{5,6},{6,7},{7,4},{8,9},{9,10},{10,1... | collective-permute-start | bytes 92168 | tf_op jit(solution)/shard_map/ppermute | solution.py:316
  20.7 5.1 %collective-permute-start.1 = (f32[4,1920]{1,0:T(4,128)S(1)}, f32[4,1920]{1,0:T(4,128)S(1)}, u32[]{:S(2)}, u32[]{:S(2)}) collective-permute-start(f32[4,1920]{1,0:T(4,128)S(1)} %bitcast.45), channel_id=1, source_target_pairs={{0,3},{1,0},{2,1},{3,2},{4,7},{5,4},{6,5},{7,6},{8,11},{9,8},{10,9... | collective-permute-start | bytes 92168 | tf_op jit(solution)/shard_map/ppermute | solution.py:317
  25.9 10.7 %all-to-all-done.in_ref = f32[16,32,128]{2,1,0:T(8,128)S(1)} async-done(((f32[16,32,128]{2,1,0:T(8,128)}), f32[16,32,128]{2,1,0:T(8,128)S(1)}, u32[]{:S(2)}, u32[]{:S(2)}) %all-to-all-start) | async-done | bytes 262176 | tf_op jit(solution)/shard_map/all_to_all | solution.py:311
  36.6 0.9 shard_map.97
  37.5 6.3 %all-to-all-start.1 = ((f32[16,32,128]{2,1,0:T(8,128)}), f32[16,32,128]{2,1,0:T(8,128)S(1)}, u32[]{:S(2)}, u32[]{:S(2)}) async-start(f32[16,32,128]{2,1,0:T(8,128)} %shard_map.97), calls=%async_computation.1 | async-start | bytes 524288 | tf_op jit(solution)/shard_map/all_to_all | solution.py:311
  43.7 0.0 collective-permute-done.left_ref
  43.7 0.0 collective-permute-done.1.right_ref
  43.8 3.6 %collective-permute-start.2 = (f32[10,1920]{1,0:T(8,128)S(1)}, f32[10,1920]{1,0:T(8,128)S(1)}, u32[]{:S(2)}, u32[]{:S(2)}) collective-permute-start(f32[10,1920]{1,0:T(8,128)S(1)} %pad_maximum_fusion), channel_id=1, source_target_pairs={{0,4},{4,8},{8,12},{12,16},{16,20},{20,24},{24,28},{1,5},{5,9},{9,... | collective-permute-start | bytes 230408 | tf_op jit(solution)/shard_map/ppermute | solution.py:321
  47.4 2.3 %collective-permute-start.3 = (f32[10,1920]{1,0:T(8,128)S(1)}, f32[10,1920]{1,0:T(8,128)S(1)}, u32[]{:S(2)}, u32[]{:S(2)}) collective-permute-start(f32[10,1920]{1,0:T(8,128)S(1)} %pad_maximum_fusion.1), channel_id=1, source_target_pairs={{4,0},{8,4},{12,8},{16,12},{20,16},{24,20},{28,24},{5,1},{9,5},{13... | collective-permute-start | bytes 230408 | tf_op jit(solution)/shard_map/ppermute | solution.py:322
  49.7 0.8 copy.13.cols_ref
  50.5 0.0 copy-start.3
  50.5 0.0 copy-start.4
  50.5 1.3 %copy.21 = bf16[1,4,8,6,1920]{4,3,2,1,0:T(8,128)(2,1)S(1)} copy(bf16[1,4,8,6,1920]{4,2,3,1,0:T(8,128)(2,1)} %param.12) | data formatting | bytes 1474560 | tf_op args[4]
  51.8 2.5 %copy.20 = bf16[1,4,8,4,6,1920]{5,4,3,2,1,0:T(8,128)(2,1)S(1)} copy(bf16[1,4,8,4,6,1920]{5,3,4,2,1,0:T(4,128)(2,1)} %param.10) | data formatting | bytes 5898240 | tf_op args[2]
  54.2 0.0 copy-start.5
  54.3 0.0 copy-start.7
  54.3 0.0 copy-start.8
  54.3 0.0 collective-permute-done.2.below_ref
  54.3 0.8 collective-permute-done.3.above_ref
  55.1 0.0 copy-done.3
  55.1 0.0 copy-done.4
  55.1 4.5 %shard_map.95.base_ref = f32[4,8,1920]{2,1,0:T(8,128)S(1)} custom-call(s32[4,8,4]{2,1,0:T(8,128)S(1)} %copy.13.cols_ref, bf16[4,8,4,6,1920]{4,3,2,1,0:T(8,128)(2,1)S(1)} %bitcast.30, f32[4,8,1920]{2,1,0:T(8,128)S(1)} %bitcast.36, f32[4,1920]{1,0:T(4,128)S(1)} %collective-permute-done.left_ref, f32[4,1920]{1,0:T(4,128)S(1)} %collective-permute-done.1.right_ref, ...), custom_call_target="tpu_custom_call" | custom-call | tf_op jit(solution)/shard_map/pallas_call | solution.py:269
  59.6 0.0 copy-start
  59.6 1.9 %copy-done = bf16[1,4,8,4,6,1920]{5,4,3,2,1,0:T(8,128)(2,1)} copy-done((bf16[1,4,8,4,6,1920]{5,4,3,2,1,0:T(8,128)(2,1)}, bf16[1,4,8,4,6,1920]{5,4,3,2,1,0:T(8,128)(2,1)S(1)}, u32[]{:S(2)}) %copy-start) | copy-done | bytes 2949144
  61.4 0.0 all-to-all-done.1
  61.5 0.0 copy-done.5
  61.5 0.0 copy-done.7
  61.5 0.0 copy-done.8
  61.5 2.4 %shard_map.98 = (f32[4,8,1920]{2,1,0:T(8,128)S(1)}, f32[512,128]{1,0:T(8,128)}, f32[4,1920]{1,0:T(4,128)S(1)}, f32[4,1920]{1,0:T(4,128)S(1)}) custom-call(f32[4,8,1920]{2,1,0:T(8,128)S(1)} %shard_map.95.base_ref, f32[512,128]{1,0:T(8,128)S(1)} %bitcast.38, f32[4,8,1920]{2,1,0:T(8,128)S(1)} %bitcast.37, bf16[4,8,6,1920]{3,2,1,0:T(8,128)(2,1)S(1)} %bitcast.32, ...), custom_call_target="tpu_custom_call" | custom-call | tf_op jit(solution)/shard_map/pallas_call | solution.py:293
  63.9 12.0 %all-to-all-start.2 = ((f32[16,32,128]{2,1,0:T(8,128)}), f32[16,32,128]{2,1,0:T(8,128)S(1)}, u32[]{:S(2)}, u32[]{:S(2)}) async-start(f32[16,32,128]{2,1,0:T(8,128)} %bitcast.12), calls=%async_computation.2 | async-start | bytes 524288 | tf_op jit(solution)/shard_map/all_to_all | solution.py:311
  75.9 1.9 %collective-permute-start.4 = (f32[4,1920]{1,0:T(4,128)S(1)}, f32[4,1920]{1,0:T(4,128)S(1)}, u32[]{:S(2)}, u32[]{:S(2)}) collective-permute-start(f32[4,1920]{1,0:T(4,128)S(1)} %get-tuple-element.9), channel_id=1, source_target_pairs={{0,1},{1,2},{2,3},{3,0},{4,5},{5,6},{6,7},{7,4},{8,9},{9,10},{10,1... | collective-permute-start | bytes 92168 | tf_op jit(solution)/shard_map/ppermute | solution.py:316
  77.8 5.1 %collective-permute-start.5 = (f32[4,1920]{1,0:T(4,128)S(1)}, f32[4,1920]{1,0:T(4,128)S(1)}, u32[]{:S(2)}, u32[]{:S(2)}) collective-permute-start(f32[4,1920]{1,0:T(4,128)S(1)} %get-tuple-element.10), channel_id=1, source_target_pairs={{0,3},{1,0},{2,1},{3,2},{4,7},{5,4},{6,5},{7,6},{8,11},{9,8},{10,9... | collective-permute-start | bytes 92168 | tf_op jit(solution)/shard_map/ppermute | solution.py:317
  83.0 10.3 %all-to-all-done.2.in_ref = f32[16,32,128]{2,1,0:T(8,128)S(1)} async-done(((f32[16,32,128]{2,1,0:T(8,128)}), f32[16,32,128]{2,1,0:T(8,128)S(1)}, u32[]{:S(2)}, u32[]{:S(2)}) %all-to-all-start.2) | async-done | bytes 262176 | tf_op jit(solution)/shard_map/all_to_all | solution.py:311
  93.3 0.9 shard_map.100
  94.2 5.0 %all-to-all-start.3 = ((f32[16,32,128]{2,1,0:T(8,128)}), f32[16,32,128]{2,1,0:T(8,128)S(1)}, u32[]{:S(2)}, u32[]{:S(2)}) async-start(f32[16,32,128]{2,1,0:T(8,128)} %shard_map.100), calls=%async_computation.3 | async-start | bytes 524288 | tf_op jit(solution)/shard_map/all_to_all | solution.py:311
  99.1 0.0 collective-permute-done.4.left_ref
  99.2 0.0 collective-permute-done.5.right_ref
  99.2 4.3 %collective-permute-start.6 = (f32[10,1920]{1,0:T(8,128)S(1)}, f32[10,1920]{1,0:T(8,128)S(1)}, u32[]{:S(2)}, u32[]{:S(2)}) collective-permute-start(f32[10,1920]{1,0:T(8,128)S(1)} %pad_maximum_fusion.2), channel_id=1, source_target_pairs={{0,4},{4,8},{8,12},{12,16},{16,20},{20,24},{24,28},{1,5},{5,9},{9,... | collective-permute-start | bytes 230408 | tf_op jit(solution)/shard_map/ppermute | solution.py:321
  103.6 1.9 %collective-permute-start.7 = (f32[10,1920]{1,0:T(8,128)S(1)}, f32[10,1920]{1,0:T(8,128)S(1)}, u32[]{:S(2)}, u32[]{:S(2)}) collective-permute-start(f32[10,1920]{1,0:T(8,128)S(1)} %pad_maximum_fusion.3), channel_id=1, source_target_pairs={{4,0},{8,4},{12,8},{16,12},{20,16},{24,20},{28,24},{5,1},{9,5},{13... | collective-permute-start | bytes 230408 | tf_op jit(solution)/shard_map/ppermute | solution.py:322
  105.5 0.5 collective-permute-done.6.below_ref
  106.0 5.3 %collective-permute-done.7.above_ref = f32[10,1920]{1,0:T(8,128)S(1)} collective-permute-done((f32[10,1920]{1,0:T(8,128)S(1)}, f32[10,1920]{1,0:T(8,128)S(1)}, u32[]{:S(2)}, u32[]{:S(2)}) %collective-permute-start.7) | collective-permute-done | bytes 76832 | tf_op jit(solution)/shard_map/ppermute | solution.py:322
  111.3 0.0 copy-start.1
  111.3 2.1 %copy-done.1 = bf16[1,4,8,4,6,1920]{5,4,3,2,1,0:T(8,128)(2,1)S(1)} copy-done((bf16[1,4,8,4,6,1920]{5,4,3,2,1,0:T(8,128)(2,1)S(1)}, bf16[1,4,8,4,6,1920]{5,4,3,2,1,0:T(8,128)(2,1)}, u32[]{:S(2)}) %copy-start.1) | copy-done | bytes 2949144
  113.4 4.5 %shard_map.99.base_ref = f32[4,8,1920]{2,1,0:T(8,128)S(1)} custom-call(s32[4,8,4]{2,1,0:T(8,128)S(1)} %copy.13.cols_ref, bf16[4,8,4,6,1920]{4,3,2,1,0:T(8,128)(2,1)S(1)} %bitcast.31, f32[4,8,1920]{2,1,0:T(8,128)S(1)} %get-tuple-element.8.state_ref, f32[4,1920]{1,0:T(4,128)S(1)} %collective-permute-done.4.left_ref, ...), custom_call_target="tpu_custom_call" | custom-call | tf_op jit(solution)/shard_map/pallas_call | solution.py:269
  117.8 0.0 all-to-all-done.3
  117.9 1.8 %shard_map.101 = (f32[4,8,1920]{2,1,0:T(8,128)}, f32[4,8,1920]{2,1,0:T(8,128)}) custom-call(f32[4,8,1920]{2,1,0:T(8,128)S(1)} %shard_map.99.base_ref, f32[512,128]{1,0:T(8,128)S(1)} %bitcast.39, f32[4,8,1920]{2,1,0:T(8,128)S(1)} %get-tuple-element.8.state_ref, bf16[4,8,6,1920]{3,2,1,0:T(8,128)(2,1)S(1)} %bitcast.33, bf16[72,256]{1,0:T(8,128)(2,1)S(1)} %bitcast.43, ...), custom_call_target="tpu_custom_call" | custom-call | tf_op jit(solution)/shard_map/pallas_call | solution.py:302
  (13 shorter events, 0.2 us)
Async XLA Ops:
  0.6 0.9 copy-start.2
  1.6 0.7 copy-start.6
  3.5 33.1 %all-to-all-start = ((f32[16,32,128]{2,1,0:T(8,128)}), f32[16,32,128]{2,1,0:T(8,128)S(1)}, u32[]{:S(2)}, u32[]{:S(2)}) async-start(f32[16,32,128]{2,1,0:T(8,128)} %bitcast.6), calls=%async_computation | async-start | bytes 524288 | tf_op jit(solution)/shard_map/all_to_all | solution.py:311
  18.7 25.0 %collective-permute-start = (f32[4,1920]{1,0:T(4,128)S(1)}, f32[4,1920]{1,0:T(4,128)S(1)}, u32[]{:S(2)}, u32[]{:S(2)}) collective-permute-start(f32[4,1920]{1,0:T(4,128)S(1)} %bitcast.44), channel_id=1, source_target_pairs={{0,1},{1,2},{2,3},{3,0},{4,5},{5,6},{6,7},{7,4},{8,9},{9,10},{10,1... | collective-permute-start | bytes 92168 | tf_op jit(solution)/shard_map/ppermute | solution.py:316
  20.7 23.0 %collective-permute-start.1 = (f32[4,1920]{1,0:T(4,128)S(1)}, f32[4,1920]{1,0:T(4,128)S(1)}, u32[]{:S(2)}, u32[]{:S(2)}) collective-permute-start(f32[4,1920]{1,0:T(4,128)S(1)} %bitcast.45), channel_id=1, source_target_pairs={{0,3},{1,0},{2,1},{3,2},{4,7},{5,4},{6,5},{7,6},{8,11},{9,8},{10,9... | collective-permute-start | bytes 92168 | tf_op jit(solution)/shard_map/ppermute | solution.py:317
  37.5 24.0 %all-to-all-start.1 = ((f32[16,32,128]{2,1,0:T(8,128)}), f32[16,32,128]{2,1,0:T(8,128)S(1)}, u32[]{:S(2)}, u32[]{:S(2)}) async-start(f32[16,32,128]{2,1,0:T(8,128)} %shard_map.97), calls=%async_computation.1 | async-start | bytes 524288 | tf_op jit(solution)/shard_map/all_to_all | solution.py:311
  43.8 10.5 %collective-permute-start.2 = (f32[10,1920]{1,0:T(8,128)S(1)}, f32[10,1920]{1,0:T(8,128)S(1)}, u32[]{:S(2)}, u32[]{:S(2)}) collective-permute-start(f32[10,1920]{1,0:T(8,128)S(1)} %pad_maximum_fusion), channel_id=1, source_target_pairs={{0,4},{4,8},{8,12},{12,16},{16,20},{20,24},{24,28},{1,5},{5,9},{9,... | collective-permute-start | bytes 230408 | tf_op jit(solution)/shard_map/ppermute | solution.py:321
  47.4 7.7 %collective-permute-start.3 = (f32[10,1920]{1,0:T(8,128)S(1)}, f32[10,1920]{1,0:T(8,128)S(1)}, u32[]{:S(2)}, u32[]{:S(2)}) collective-permute-start(f32[10,1920]{1,0:T(8,128)S(1)} %pad_maximum_fusion.1), channel_id=1, source_target_pairs={{4,0},{8,4},{12,8},{16,12},{20,16},{24,20},{28,24},{5,1},{9,5},{13... | collective-permute-start | bytes 230408 | tf_op jit(solution)/shard_map/ppermute | solution.py:322
  50.5 4.6 %copy-start.3 = (f32[1,4,8,1920]{3,2,1,0:T(8,128)S(1)}, f32[1,4,8,1920]{3,2,1,0:T(8,128)}, u32[]{:S(2)}) copy-start(f32[1,4,8,1920]{3,2,1,0:T(8,128)} %param.9) | copy-start | bytes 737284
  50.5 4.6 %copy-start.4 = (f32[1,4,8,1920]{3,2,1,0:T(8,128)S(1)}, f32[1,4,8,1920]{3,2,1,0:T(8,128)}, u32[]{:S(2)}) copy-start(f32[1,4,8,1920]{3,2,1,0:T(8,128)} %param.8) | copy-start | bytes 737284
  54.2 7.2 %copy-start.5 = (bf16[1,72,256]{2,1,0:T(8,128)(2,1)S(1)}, bf16[1,72,256]{2,1,0:T(8,128)(2,1)}, u32[]{:S(2)}) copy-start(bf16[1,72,256]{2,1,0:T(8,128)(2,1)} %param.15) | copy-start | bytes 110596
  54.3 7.2 %copy-start.7 = (s32[2,256]{1,0:T(2,128)S(1)}, s32[2,256]{1,0:T(2,128)}, u32[]{:S(2)}) copy-start(s32[2,256]{1,0:T(2,128)} %src_ref.3) | copy-start | bytes 6148
  54.3 7.2 %copy-start.8 = (s32[2,256]{1,0:T(2,128)S(1)}, s32[2,256]{1,0:T(2,128)}, u32[]{:S(2)}) copy-start(s32[2,256]{1,0:T(2,128)} %dst_ref.3) | copy-start | bytes 6148
  59.6 1.9 %copy-start = (bf16[1,4,8,4,6,1920]{5,4,3,2,1,0:T(8,128)(2,1)}, bf16[1,4,8,4,6,1920]{5,4,3,2,1,0:T(8,128)(2,1)S(1)}, u32[]{:S(2)}) copy-start(bf16[1,4,8,4,6,1920]{5,4,3,2,1,0:T(8,128)(2,1)S(1)} %copy.20) | copy-start | bytes 8847364
  63.9 29.4 %all-to-all-start.2 = ((f32[16,32,128]{2,1,0:T(8,128)}), f32[16,32,128]{2,1,0:T(8,128)S(1)}, u32[]{:S(2)}, u32[]{:S(2)}) async-start(f32[16,32,128]{2,1,0:T(8,128)} %bitcast.12), calls=%async_computation.2 | async-start | bytes 524288 | tf_op jit(solution)/shard_map/all_to_all | solution.py:311
  75.9 23.3 %collective-permute-start.4 = (f32[4,1920]{1,0:T(4,128)S(1)}, f32[4,1920]{1,0:T(4,128)S(1)}, u32[]{:S(2)}, u32[]{:S(2)}) collective-permute-start(f32[4,1920]{1,0:T(4,128)S(1)} %get-tuple-element.9), channel_id=1, source_target_pairs={{0,1},{1,2},{2,3},{3,0},{4,5},{5,6},{6,7},{7,4},{8,9},{9,10},{10,1... | collective-permute-start | bytes 92168 | tf_op jit(solution)/shard_map/ppermute | solution.py:316
  77.8 21.4 %collective-permute-start.5 = (f32[4,1920]{1,0:T(4,128)S(1)}, f32[4,1920]{1,0:T(4,128)S(1)}, u32[]{:S(2)}, u32[]{:S(2)}) collective-permute-start(f32[4,1920]{1,0:T(4,128)S(1)} %get-tuple-element.10), channel_id=1, source_target_pairs={{0,3},{1,0},{2,1},{3,2},{4,7},{5,4},{6,5},{7,6},{8,11},{9,8},{10,9... | collective-permute-start | bytes 92168 | tf_op jit(solution)/shard_map/ppermute | solution.py:317
  94.2 23.7 %all-to-all-start.3 = ((f32[16,32,128]{2,1,0:T(8,128)}), f32[16,32,128]{2,1,0:T(8,128)S(1)}, u32[]{:S(2)}, u32[]{:S(2)}) async-start(f32[16,32,128]{2,1,0:T(8,128)} %shard_map.100), calls=%async_computation.3 | async-start | bytes 524288 | tf_op jit(solution)/shard_map/all_to_all | solution.py:311
  99.2 6.8 %collective-permute-start.6 = (f32[10,1920]{1,0:T(8,128)S(1)}, f32[10,1920]{1,0:T(8,128)S(1)}, u32[]{:S(2)}, u32[]{:S(2)}) collective-permute-start(f32[10,1920]{1,0:T(8,128)S(1)} %pad_maximum_fusion.2), channel_id=1, source_target_pairs={{0,4},{4,8},{8,12},{12,16},{16,20},{20,24},{24,28},{1,5},{5,9},{9,... | collective-permute-start | bytes 230408 | tf_op jit(solution)/shard_map/ppermute | solution.py:321
  103.6 7.7 %collective-permute-start.7 = (f32[10,1920]{1,0:T(8,128)S(1)}, f32[10,1920]{1,0:T(8,128)S(1)}, u32[]{:S(2)}, u32[]{:S(2)}) collective-permute-start(f32[10,1920]{1,0:T(8,128)S(1)} %pad_maximum_fusion.3), channel_id=1, source_target_pairs={{4,0},{8,4},{12,8},{16,12},{20,16},{24,20},{28,24},{5,1},{9,5},{13... | collective-permute-start | bytes 230408 | tf_op jit(solution)/shard_map/ppermute | solution.py:322
  111.3 2.1 %copy-start.1 = (bf16[1,4,8,4,6,1920]{5,4,3,2,1,0:T(8,128)(2,1)S(1)}, bf16[1,4,8,4,6,1920]{5,4,3,2,1,0:T(8,128)(2,1)}, u32[]{:S(2)}) copy-start(bf16[1,4,8,4,6,1920]{5,4,3,2,1,0:T(8,128)(2,1)} %copy-done) | copy-start | bytes 8847364
where the time goes:
time: 121 us; the launch traced here: 120 us
  starting transfers between devices  64.7 us (53%)
  waiting for transfers between devices  27.6 us (23%)
  Pallas kernels  16.1 us (13%)
  local copies, waits for them, and re-layouts  10.3 us (9%)
    all_to_all x4, starting transfers between devices, exchange(): return lax.all_to_all(array, 'inst', 0, 0, tiled=True)  38.5 us
    all_to_all x4, waiting for transfers between devices, exchange(): return lax.all_to_all(array, 'inst', 0, 0, tiled=True)  21 us
    ppermute x2, starting transfers between devices, halos(): lax.ppermute(high_edge, 'chord', [(i, (i - 1) % n) for i in range(n)])  10.3 us
    unnamed x23, local copies, waits for them, and re-layouts  10.2 us
    pallas_call x2, Pallas kernels, tile_call(): pl.pallas_call(tile_kernel, out_shape=STATE, grid=(SB,), in_specs=[pl.Blo...  8.93 us
    ppermute x2, starting transfers between devices, halos(): below = lax.ppermute(last, 'span', [(i, i + 1) for i in range(n - 1)])  7.9 us
    ppermute x2, waiting for transfers between devices, halos(): above = lax.ppermute(first, 'span', [(i + 1, i) for i in range(n - 1)])  6.04 us
    ppermute x2, starting transfers between devices, halos(): above = lax.ppermute(first, 'span', [(i + 1, i) for i in range(n - 1)])  4.18 us
  transfers between devices with their start and end apart: 12, of which 5 were waited for; matrix products, arithmetic and copies ran while one was open for 4% of the time, Pallas kernels for 9%

commit v1 on v0

--- a/solution.py
+++ b/solution.py
@@ -95,8 +95,17 @@
         high_ref[p : p + 1, :] = state_ref[p, 0:1, :]
 
 
-def start_kernel(state_ref, src_ref, send_ref):
-    emit_exchange(state_ref, src_ref, send_ref)
+def start_kernel(state_ref, src_ref, send_ref, low_ref, high_ref, state, src, sems):
+    copies = [
+        pltpu.make_async_copy(state_ref, state, sems.at[0]),
+        pltpu.make_async_copy(src_ref, src, sems.at[1]),
+    ]
+    for copy in copies:
+        copy.start()
+    for copy in copies:
+        copy.wait()
+    emit_exchange(state, src, send_ref)
+    emit_edges(state, low_ref, high_ref)
 
 
 def spectral_kernel(who_ref, in_ref, out_ref):
@@ -127,12 +136,6 @@
             out_ref[t, 16:32, :] = in_ref[(t + LAG) % NT, 16:32, :]
 
 
-def fold(product):
-    pair = 2 * BLK
-    total = product[:, :pair] + product[:, pair : 2 * pair] + product[:, 2 * pair :]
-    return total[:, :BLK] + total[:, BLK:]
-
-
 def put(ref, row, count, value):
     ref[0, pl.ds(row, count), :] = value[:, :LANES]
     ref[1, pl.ds(row, count), :] = value[:, LANES : 2 * LANES]
@@ -144,41 +147,63 @@
     return jnp.concatenate(parts, axis=1)[:, :BLK]
 
 
+def fold_pair(total):
+    return total[:, :BLK] + total[:, BLK:]
+
+
+def sum_pairs(product):
+    pair = 2 * BLK
+    return product[:, :pair] + product[:, pair : 2 * pair] + product[:, 2 * pair :]
+
+
 def tile_kernel(
-    cols_ref, tiles_ref, state_ref, left_ref, right_ref, below_ref, above_ref, source_ref, out_ref, wide, term
+    cols_ref, tiles_hbm, state_ref, left_ref, right_ref, below_ref, above_ref, source_ref, out_ref, tiles_ref, wide, chosen, partial, sems
 ):
-    p = pl.program_id(0)
-
-    @pl.when(p == 0)
-    def _():
-        wide[0:10, :] = below_ref[...]
-        wide[(SB + 1) * 16 : (SB + 1) * 16 + 10, :] = above_ref[...]
-        for row in range(SB):
-            base = (row + 1) * 16
-            wide[base : base + 8, :] = state_ref[row]
-            wide[base + 8 : base + 9, :] = left_ref[row : row + 1, :]
-            wide[base + 9 : base + 10, :] = right_ref[row : row + 1, :]
-
-    def block(q, carry):
-        total = None
-        for k in range(K):
-            code = cols_ref[p, q, k]
-            a = lax.div(code, 3)
-            side = q + code - 3 * a - 1
-            column = jnp.where(side < 0, CB, jnp.where(side == CB, CB + 1, side))
-            row = (p + a) * 16 + column
-            product = tiles_ref[0, q, k].astype(jnp.float32) * wide[pl.ds(row, 1), :]
-            total = product if total is None else total + product
-        put(term, pl.multiple_of(q * 8, 8), NV, fold(total))
+    def fetch(p):
+        return pltpu.make_async_copy(tiles_hbm.at[p], tiles_ref.at[p], sems.at[p])
+
+    for p in range(SB):
+        fetch(p).start()
+    wide[0:10, :] = below_ref[...]
+    wide[(SB + 1) * 16 : (SB + 1) * 16 + 10, :] = above_ref[...]
+    for row in range(SB):
+        base = (row + 1) * 16
+        wide[base : base + 8, :] = state_ref[row]
+        wide[base + 8 : base + 9, :] = left_ref[row : row + 1, :]
+        wide[base + 9 : base + 10, :] = right_ref[row : row + 1, :]
+
+    def block_row(p, carry):
+        fetch(p).wait()
+        for q in range(CB):
+            for k in range(K):
+                code = cols_ref[p, k, q]
+                a = lax.shift_right_logical(code * 11, 5)
+                side = q + code - 3 * a - 1
+                column = jnp.where(side < 0, CB, jnp.where(side == CB, CB + 1, side))
+                row = (p + a) * 16 + column
+                chosen[q * 8 + k : q * 8 + k + 1, :] = wide[pl.ds(row, 1), :]
+            inputs = chosen[q * 8 : q * 8 + K, :]
+            for v in range(NV):
+                total = sum_pairs(tiles_ref[p, q, v].astype(jnp.float32) * inputs)
+                for n in range(2 * BLK // LANES):
+                    at = v * CB * K + q * K
+                    partial[n, at : at + K, :] = total[:, n * LANES : (n + 1) * LANES]
+        for v in range(NV):
+            lanes = slice(v * BLK, (v + 1) * BLK)
+            total = None
+            for k in range(K):
+                rows = pl.ds(v * CB * K + k, CB, stride=K)
+                one = jnp.concatenate([partial[n, rows, :] for n in range(2 * BLK // LANES)], axis=1)
+                total = one if total is None else total + one
+            out_ref[p, :, lanes] = source_ref[p, :, lanes] - fold_pair(total)
         return carry
 
-    lax.fori_loop(0, CB, block, 0)
-    for v in range(NV):
-        lanes = slice(v * BLK, (v + 1) * BLK)
-        out_ref[0, :, lanes] = source_ref[0, :, lanes] - take(term, v)
-
-
-def finish(base_ref, spectral_ref, state_ref, inverse_ref, coef_ref, dst_ref, residual_ref, next_ref, lagged, term):
+    lax.fori_loop(0, SB, block_row, 0)
+
+
+def finish(base_ref, spectral_ref, state_ref, inverse_hbm, coef_ref, dst_ref, residual_ref, next_ref, lagged, inverse_ref, sem):
+    fetch = pltpu.make_async_copy(inverse_hbm, inverse_ref, sem)
+    fetch.start()
     coef = coef_ref[...].astype(jnp.float32)
     spread, cells = [], []
     for side in range(2):
@@ -203,6 +228,7 @@
     )
     count = SB * CB * 8
     put(lagged, 0, count, placed[:count] + (placed[count : 2 * count] + placed[2 * count :]))
+    fetch.wait()
     for p in range(SB):
         first = p * STRIPS * 8
         spectral = jnp.concatenate(
@@ -215,29 +241,24 @@
                 residual_ref[p, :, lanes] - take(lagged, p * CB * 8 + v)
             )
 
-        def block(q, carry):
-            product = inverse_ref[p, q].astype(jnp.float32) * residual_ref[p, pl.ds(q, 1), :]
-            put(term, pl.multiple_of(q * 8, 8), NV, fold(product))
-            return carry
-
-        lax.fori_loop(0, CB, block, 0, unroll=True)
         for v in range(NV):
             lanes = slice(v * BLK, (v + 1) * BLK)
-            next_ref[p, :, lanes] = state_ref[p, :, lanes] + take(term, v)
+            product = inverse_ref[p, v].astype(jnp.float32) * residual_ref[p]
+            next_ref[p, :, lanes] = state_ref[p, :, lanes] + fold_pair(sum_pairs(product))
 
 
 def middle_kernel(
-    base_ref, spectral_ref, state_ref, inverse_ref, coef_ref, dst_ref, src_ref, next_ref, send_ref, low_ref, high_ref, residual_ref, lagged, term
+    base_ref, spectral_ref, state_ref, inverse_hbm, coef_ref, dst_ref, src_ref, next_ref, send_ref, low_ref, high_ref, residual_ref, lagged, inverse, sem
 ):
-    finish(base_ref, spectral_ref, state_ref, inverse_ref, coef_ref, dst_ref, residual_ref, next_ref, lagged, term)
+    finish(base_ref, spectral_ref, state_ref, inverse_hbm, coef_ref, dst_ref, residual_ref, next_ref, lagged, inverse, sem)
     emit_exchange(next_ref, src_ref, send_ref)
     emit_edges(next_ref, low_ref, high_ref)
 
 
 def last_kernel(
-    base_ref, spectral_ref, state_ref, inverse_ref, coef_ref, dst_ref, next_ref, residual_ref, lagged, term
+    base_ref, spectral_ref, state_ref, inverse_hbm, coef_ref, dst_ref, next_ref, residual_ref, lagged, inverse, sem
 ):
-    finish(base_ref, spectral_ref, state_ref, inverse_ref, coef_ref, dst_ref, residual_ref, next_ref, lagged, term)
+    finish(base_ref, spectral_ref, state_ref, inverse_hbm, coef_ref, dst_ref, residual_ref, next_ref, lagged, inverse, sem)
 
 
 def f32(*shape):
@@ -247,12 +268,31 @@
 STATE = f32(SB, CB, WIDTH)
 EDGE = f32(SB, WIDTH)
 SEND = f32(NT * SHARE, LANES)
-FINISH_SCRATCH = [pltpu.VMEM((3, SB * CB * 8, LANES), jnp.float32), pltpu.VMEM((3, CB * 8, LANES), jnp.float32)]
-ROOM = pltpu.CompilerParams(vmem_limit_bytes=32 << 20)
+FINISH_SCRATCH = [
+    pltpu.VMEM((3, SB * CB * 8, LANES), jnp.float32),
+    pltpu.VMEM((SB, NV, CB, WIDTH), jnp.bfloat16),
+    pltpu.SemaphoreType.DMA,
+]
+def room(mebibytes):
+    return pltpu.CompilerParams(vmem_limit_bytes=mebibytes << 20)
+
+
+def in_hbm(array):
+    return pltpu.with_memory_space_constraint(array, pltpu.HBM)
 
 
 def start_call(state, src):
-    return pl.pallas_call(start_kernel, out_shape=SEND, compiler_params=ROOM)(state, src)
+    return pl.pallas_call(
+        start_kernel,
+        out_shape=(SEND, EDGE, EDGE),
+        in_specs=[pl.BlockSpec(memory_space=pltpu.HBM)] * 2,
+        scratch_shapes=[
+            pltpu.VMEM(state.shape, state.dtype),
+            pltpu.VMEM(src.shape, src.dtype),
+            pltpu.SemaphoreType.DMA((2,)),
+        ],
+        compiler_params=room(8),
+    )(in_hbm(state), in_hbm(src))
 
 
 def spectral_call(who, received):
@@ -260,51 +300,51 @@
         spectral_kernel,
         out_shape=f32(NT, SHARE, LANES),
         in_specs=[pl.BlockSpec(memory_space=pltpu.SMEM), pl.BlockSpec(memory_space=pltpu.VMEM)],
-        compiler_params=ROOM,
+        compiler_params=room(4),
     )(who, received)
 
 
 def tile_call(cols, tiles, state, left, right, below, above, source):
-    whole = lambda array: pl.BlockSpec(array.shape, lambda p: (0,) * array.ndim)
+    in_vmem = pl.BlockSpec(memory_space=pltpu.VMEM)
     return pl.pallas_call(
         tile_kernel,
         out_shape=STATE,
-        grid=(SB,),
-        in_specs=[
-            pl.BlockSpec(memory_space=pltpu.SMEM),
-            pl.BlockSpec((1, CB, K, NV, WIDTH), lambda p: (p, 0, 0, 0, 0)),
-            whole(state),
-            whole(left),
-            whole(right),
-            whole(below),
-            whole(above),
-            pl.BlockSpec((1, CB, WIDTH), lambda p: (p, 0, 0)),
+        in_specs=[pl.BlockSpec(memory_space=pltpu.SMEM), pl.BlockSpec(memory_space=pltpu.HBM)] + [in_vmem] * 6,
+        scratch_shapes=[
+            pltpu.VMEM(tiles.shape, tiles.dtype),
+            pltpu.VMEM(((SB + 2) * 16, WIDTH), jnp.float32),
+            pltpu.VMEM((CB * 8, WIDTH), jnp.float32),
+            pltpu.VMEM((2 * BLK // LANES, NV * CB * K, LANES), jnp.float32),
+            pltpu.SemaphoreType.DMA((SB,)),
         ],
-        out_specs=pl.BlockSpec((1, CB, WIDTH), lambda p: (p, 0, 0)),
-        scratch_shapes=[
-            pltpu.VMEM(((SB + 2) * 16, WIDTH), jnp.float32),
-            pltpu.VMEM((3, CB * 8, LANES), jnp.float32),
-        ],
-        compiler_params=ROOM,
-    )(cols, tiles, state, left, right, below, above, source)
+        compiler_params=room(8),
+    )(cols, in_hbm(tiles), state, left, right, below, above, source)
+
+
+def finish_specs(count):
+    specs = [pl.BlockSpec(memory_space=pltpu.VMEM)] * count
+    specs[3] = pl.BlockSpec(memory_space=pltpu.HBM)
+    return specs
 
 
 def middle_call(base, spectral, state, inverse, coef, dst, src):
     return pl.pallas_call(
         middle_kernel,
         out_shape=(STATE, SEND, EDGE, EDGE),
+        in_specs=finish_specs(7),
         scratch_shapes=[pltpu.VMEM((SB, CB, WIDTH), jnp.float32)] + FINISH_SCRATCH,
-        compiler_params=ROOM,
-    )(base, spectral, state, inverse, coef, dst, src)
+        compiler_params=room(8),
+    )(base, spectral, state, in_hbm(inverse), coef, dst, src)
 
 
 def last_call(base, spectral, state, inverse, coef, dst):
     return pl.pallas_call(
         last_kernel,
         out_shape=(STATE, STATE),
+        in_specs=finish_specs(6),
         scratch_shapes=FINISH_SCRATCH,
-        compiler_params=ROOM,
-    )(base, spectral, state, inverse, coef, dst)
+        compiler_params=room(8),
+    )(base, spectral, state, in_hbm(inverse), coef, dst)
 
 
 def exchange(array):
@@ -325,10 +365,12 @@
 
 def per_device(adj_source, adj_start, tiles, tile_cols, inverse_diag, face_src, face_dst, lag_coef):
     source, state = adj_source[0], adj_start[0]
-    tiles, inverse, coef = tiles[0], inverse_diag[0], lag_coef[0]
+    tiles = tiles[0].transpose(0, 1, 3, 2, 4)
+    inverse = inverse_diag[0].transpose(0, 2, 1, 3)
+    tile_cols = tile_cols.transpose(0, 2, 1)
+    coef = lag_coef[0]
     who = lax.axis_index("inst").astype(jnp.int32)[None]
-    send = start_call(state, face_src)
-    low_edge, high_edge = state[:, CB - 1], state[:, 0]
+    send, low_edge, high_edge = start_call(state, face_src)
     for sweep in range(SWEEPS):
         received = exchange(send.reshape(NT, SHARE, LANES))
         left, right, below, above = halos(state, low_edge, high_edge)

time: 121 us -> 120 us (level)
  the two profiles are of different devices: /device:TPU:58 before, /device:TPU:22 now
where the time goes in v1:
time: 120 us; the launch traced here: 119 us
  starting transfers between devices  64.5 us (54%)
  waiting for transfers between devices  33.7 us (28%)
  Pallas kernels  16.4 us (14%)
  local copies, waits for them, and re-layouts  3.55 us (3%)
    all_to_all x4, starting transfers between devices, exchange(): return lax.all_to_all(array, 'inst', 0, 0, tiled=True)  36.8 us
    all_to_all x4, waiting for transfers between devices, exchange(): return lax.all_to_all(array, 'inst', 0, 0, tiled=True)  27.5 us
    ppermute x2, starting transfers between devices, halos(): lax.ppermute(high_edge, 'chord', [(i, (i - 1) % n) for i in range(n)])  10.3 us
    ppermute x2, starting transfers between devices, halos(): above = lax.ppermute(first, 'span', [(i + 1, i) for i in range(n - 1)])  8.37 us
    pallas_call x2, Pallas kernels, tile_call(): pl.pallas_call(tile_kernel, out_shape=STATE, in_specs=[pl.BlockSpec(memor...  7.22 us
    ppermute x2, starting transfers between devices, halos(): below = lax.ppermute(last, 'span', [(i, i + 1) for i in range(n - 1)])  5.11 us
    ppermute x2, waiting for transfers between devices, halos(): above = lax.ppermute(first, 'span', [(i + 1, i) for i in range(n - 1)])  4.28 us
    ppermute x2, starting transfers between devices, halos(): left = lax.ppermute(low_edge, 'chord', [(i, (i + 1) % n) for i in range(n)])  3.97 us
  transfers between devices with their start and end apart: 12, of which 8 were waited for; matrix products, arithmetic and copies ran while one was open for 1% of the time, Pallas kernels for 7%

profile of v1, /device:TPU:22, one launch (start us, length us, event | category | flops | bytes accessed | tf_op | source)
XLA Modules:
  0.0 119.2 jit_solution(12873484822128474711)
XLA Ops:
  0.6 2.2 %shard_map.95 = (f32[512,128]{1,0:T(8,128)}, f32[4,1920]{1,0:T(4,128)S(1)}, f32[4,1920]{1,0:T(4,128)S(1)}) custom-call(f32[4,8,1920]{2,1,0:T(8,128)} %bitcast.25, s32[2,256]{1,0:T(2,128)} %src_ref.3), custom_call_target="tpu_custom_call" | custom-call | tf_op jit(solution)/shard_map/pallas_call | solution.py:285
  2.8 15.2 %all-to-all-start = ((f32[16,32,128]{2,1,0:T(8,128)}), f32[16,32,128]{2,1,0:T(8,128)S(1)}, u32[]{:S(2)}, u32[]{:S(2)}) async-start(f32[16,32,128]{2,1,0:T(8,128)} %bitcast.9), calls=%async_computation | async-start | bytes 524288 | tf_op jit(solution)/shard_map/all_to_all | solution.py:351
  18.0 0.0 copy-start.1
  18.1 0.0 copy-start.4
  18.1 0.0 copy-start.7
  18.1 0.0 copy-start.8
  18.1 2.1 %collective-permute-start = (f32[4,1920]{1,0:T(4,128)S(1)}, f32[4,1920]{1,0:T(4,128)S(1)}, u32[]{:S(2)}, u32[]{:S(2)}) collective-permute-start(f32[4,1920]{1,0:T(4,128)S(1)} %get-tuple-element.11), channel_id=1, source_target_pairs={{0,1},{1,2},{2,3},{3,0},{4,5},{5,6},{6,7},{7,4},{8,9},{9,10},{10,1... | collective-permute-start | bytes 92168 | tf_op jit(solution)/shard_map/ppermute | solution.py:356
  20.2 5.1 %collective-permute-start.1 = (f32[4,1920]{1,0:T(4,128)S(1)}, f32[4,1920]{1,0:T(4,128)S(1)}, u32[]{:S(2)}, u32[]{:S(2)}) collective-permute-start(f32[4,1920]{1,0:T(4,128)S(1)} %get-tuple-element.12), channel_id=1, source_target_pairs={{0,3},{1,0},{2,1},{3,2},{4,7},{5,4},{6,5},{7,6},{8,11},{9,8},{10,9... | collective-permute-start | bytes 92168 | tf_op jit(solution)/shard_map/ppermute | solution.py:357
  25.3 0.9 slice_bitcast_fusion.2
  26.2 10.2 %all-to-all-done.in_ref = f32[16,32,128]{2,1,0:T(8,128)S(1)} async-done(((f32[16,32,128]{2,1,0:T(8,128)}), f32[16,32,128]{2,1,0:T(8,128)S(1)}, u32[]{:S(2)}, u32[]{:S(2)}) %all-to-all-start) | async-done | bytes 262176 | tf_op jit(solution)/shard_map/all_to_all | solution.py:351
  36.4 0.8 shard_map.97
  37.3 5.8 %all-to-all-start.1 = ((f32[16,32,128]{2,1,0:T(8,128)}), f32[16,32,128]{2,1,0:T(8,128)S(1)}, u32[]{:S(2)}, u32[]{:S(2)}) async-start(f32[16,32,128]{2,1,0:T(8,128)} %shard_map.97), calls=%async_computation.1 | async-start | bytes 524288 | tf_op jit(solution)/shard_map/all_to_all | solution.py:351
  43.1 0.0 collective-permute-done.left_ref
  43.1 0.0 collective-permute-done.1.right_ref
  43.1 3.2 %collective-permute-start.2 = (f32[10,1920]{1,0:T(8,128)S(1)}, f32[10,1920]{1,0:T(8,128)S(1)}, u32[]{:S(2)}, u32[]{:S(2)}) collective-permute-start(f32[10,1920]{1,0:T(8,128)S(1)} %pad_maximum_fusion), channel_id=1, source_target_pairs={{0,4},{4,8},{8,12},{12,16},{16,20},{20,24},{24,28},{1,5},{5,9},{9,... | collective-permute-start | bytes 230408 | tf_op jit(solution)/shard_map/ppermute | solution.py:361
  46.4 3.6 %collective-permute-start.3 = (f32[10,1920]{1,0:T(8,128)S(1)}, f32[10,1920]{1,0:T(8,128)S(1)}, u32[]{:S(2)}, u32[]{:S(2)}) collective-permute-start(f32[10,1920]{1,0:T(8,128)S(1)} %pad_maximum_fusion.1), channel_id=1, source_target_pairs={{4,0},{8,4},{12,8},{16,12},{20,16},{24,20},{28,24},{5,1},{9,5},{13... | collective-permute-start | bytes 230408 | tf_op jit(solution)/shard_map/ppermute | solution.py:362
  49.9 1.0 collective-permute-done.2.below_ref
  50.9 2.6 %collective-permute-done.3.above_ref = f32[10,1920]{1,0:T(8,128)S(1)} collective-permute-done((f32[10,1920]{1,0:T(8,128)S(1)}, f32[10,1920]{1,0:T(8,128)S(1)}, u32[]{:S(2)}, u32[]{:S(2)}) %collective-permute-start.3) | collective-permute-done | bytes 76832 | tf_op jit(solution)/shard_map/ppermute | solution.py:362
  53.4 0.0 copy-start
  53.5 0.9 copy-done
  54.4 0.0 copy-start.2
  54.4 0.9 copy-done.2
  55.3 0.0 copy-start.5
  55.3 0.7 copy-done.5
  56.0 0.0 copy-start.3
  56.0 0.0 copy-start.6
  56.0 3.6 %shard_map.96.base_ref = f32[4,8,1920]{2,1,0:T(8,128)S(1)} custom-call(s32[4,4,8]{2,1,0:T(4,128)S(1)} %bitcast.34, bf16[4,8,6,4,1920]{4,3,2,1,0:T(4,128)(2,1)} %bitcast.36, f32[4,8,1920]{2,1,0:T(8,128)S(1)} %bitcast.26, f32[4,1920]{1,0:T(4,128)S(1)} %collective-permute-done.left_ref, f32[4,1920]{1,0:T(4,128)S(1)} %collective-permute-done.1.right_ref, ...), custom_call_target="tpu_custom_call" | custom-call | tf_op jit(solution)/shard_map/pallas_call | solution.py:309
  59.7 1.8 %all-to-all-done.1 = f32[16,32,128]{2,1,0:T(8,128)S(1)} async-done(((f32[16,32,128]{2,1,0:T(8,128)}), f32[16,32,128]{2,1,0:T(8,128)S(1)}, u32[]{:S(2)}, u32[]{:S(2)}) %all-to-all-start.1) | async-done | bytes 262176 | tf_op jit(solution)/shard_map/all_to_all | solution.py:351
  61.5 0.0 copy-done.1
  61.5 0.0 copy-done.4
  61.5 0.0 copy-done.7
  61.5 0.0 copy-done.8
  61.5 2.9 %shard_map.98 = (f32[4,8,1920]{2,1,0:T(8,128)S(1)}, f32[512,128]{1,0:T(8,128)}, f32[4,1920]{1,0:T(4,128)S(1)}, f32[4,1920]{1,0:T(4,128)S(1)}) custom-call(f32[4,8,1920]{2,1,0:T(8,128)S(1)} %shard_map.96.base_ref, f32[512,128]{1,0:T(8,128)S(1)} %bitcast.28, f32[4,8,1920]{2,1,0:T(8,128)S(1)} %bitcast.27, bf16[4,6,8,1920]{3,2,1,0:T(8,128)(2,1)} %bitcast.38, ...), custom_call_target="tpu_custom_call" | custom-call | tf_op jit(solution)/shard_map/pallas_call | solution.py:331
  64.4 10.3 %all-to-all-start.2 = ((f32[16,32,128]{2,1,0:T(8,128)}), f32[16,32,128]{2,1,0:T(8,128)S(1)}, u32[]{:S(2)}, u32[]{:S(2)}) async-start(f32[16,32,128]{2,1,0:T(8,128)} %bitcast.16), calls=%async_computation.2 | async-start | bytes 524288 | tf_op jit(solution)/shard_map/all_to_all | solution.py:351
  74.7 1.9 %collective-permute-start.4 = (f32[4,1920]{1,0:T(4,128)S(1)}, f32[4,1920]{1,0:T(4,128)S(1)}, u32[]{:S(2)}, u32[]{:S(2)}) collective-permute-start(f32[4,1920]{1,0:T(4,128)S(1)} %get-tuple-element.15), channel_id=1, source_target_pairs={{0,1},{1,2},{2,3},{3,0},{4,5},{5,6},{6,7},{7,4},{8,9},{9,10},{10,1... | collective-permute-start | bytes 92168 | tf_op jit(solution)/shard_map/ppermute | solution.py:356
  76.6 5.1 %collective-permute-start.5 = (f32[4,1920]{1,0:T(4,128)S(1)}, f32[4,1920]{1,0:T(4,128)S(1)}, u32[]{:S(2)}, u32[]{:S(2)}) collective-permute-start(f32[4,1920]{1,0:T(4,128)S(1)} %get-tuple-element.16), channel_id=1, source_target_pairs={{0,3},{1,0},{2,1},{3,2},{4,7},{5,4},{6,5},{7,6},{8,11},{9,8},{10,9... | collective-permute-start | bytes 92168 | tf_op jit(solution)/shard_map/ppermute | solution.py:357
  81.8 10.7 %all-to-all-done.2.in_ref = f32[16,32,128]{2,1,0:T(8,128)S(1)} async-done(((f32[16,32,128]{2,1,0:T(8,128)}), f32[16,32,128]{2,1,0:T(8,128)S(1)}, u32[]{:S(2)}, u32[]{:S(2)}) %all-to-all-start.2) | async-done | bytes 262176 | tf_op jit(solution)/shard_map/all_to_all | solution.py:351
  92.5 0.8 shard_map.100
  93.3 5.5 %all-to-all-start.3 = ((f32[16,32,128]{2,1,0:T(8,128)}), f32[16,32,128]{2,1,0:T(8,128)S(1)}, u32[]{:S(2)}, u32[]{:S(2)}) async-start(f32[16,32,128]{2,1,0:T(8,128)} %shard_map.100), calls=%async_computation.3 | async-start | bytes 524288 | tf_op jit(solution)/shard_map/all_to_all | solution.py:351
  98.9 0.0 collective-permute-done.4.left_ref
  98.9 0.0 collective-permute-done.5.right_ref
  99.0 1.9 %collective-permute-start.6 = (f32[10,1920]{1,0:T(8,128)S(1)}, f32[10,1920]{1,0:T(8,128)S(1)}, u32[]{:S(2)}, u32[]{:S(2)}) collective-permute-start(f32[10,1920]{1,0:T(8,128)S(1)} %pad_maximum_fusion.2), channel_id=1, source_target_pairs={{0,4},{4,8},{8,12},{12,16},{16,20},{20,24},{24,28},{1,5},{5,9},{9,... | collective-permute-start | bytes 230408 | tf_op jit(solution)/shard_map/ppermute | solution.py:361
  100.9 4.8 %collective-permute-start.7 = (f32[10,1920]{1,0:T(8,128)S(1)}, f32[10,1920]{1,0:T(8,128)S(1)}, u32[]{:S(2)}, u32[]{:S(2)}) collective-permute-start(f32[10,1920]{1,0:T(8,128)S(1)} %pad_maximum_fusion.3), channel_id=1, source_target_pairs={{4,0},{8,4},{12,8},{16,12},{20,16},{24,20},{28,24},{5,1},{9,5},{13... | collective-permute-start | bytes 230408 | tf_op jit(solution)/shard_map/ppermute | solution.py:362
  105.7 1.0 collective-permute-done.6.below_ref
  106.7 1.7 %collective-permute-done.7.above_ref = f32[10,1920]{1,0:T(8,128)S(1)} collective-permute-done((f32[10,1920]{1,0:T(8,128)S(1)}, f32[10,1920]{1,0:T(8,128)S(1)}, u32[]{:S(2)}, u32[]{:S(2)}) %collective-permute-start.7) | collective-permute-done | bytes 76832 | tf_op jit(solution)/shard_map/ppermute | solution.py:362
  108.5 0.0 copy-done.3
  108.5 0.0 copy-done.6
  108.5 3.6 %shard_map.99.base_ref = f32[4,8,1920]{2,1,0:T(8,128)S(1)} custom-call(s32[4,4,8]{2,1,0:T(4,128)S(1)} %bitcast.35, bf16[4,8,6,4,1920]{4,3,2,1,0:T(4,128)(2,1)} %bitcast.37, f32[4,8,1920]{2,1,0:T(8,128)S(1)} %get-tuple-element.14.state_ref, f32[4,1920]{1,0:T(4,128)S(1)} %collective-permute-done.4.left_ref, f32[4,1920]{1,0:T(4,128)S(1)} %collective-permute-done.5.right_ref, ...), custom_call_target="tpu_custom_call" | custom-call | tf_op jit(solution)/shard_map/pallas_call | solution.py:309
  112.1 4.7 %all-to-all-done.3 = f32[16,32,128]{2,1,0:T(8,128)S(1)} async-done(((f32[16,32,128]{2,1,0:T(8,128)}), f32[16,32,128]{2,1,0:T(8,128)S(1)}, u32[]{:S(2)}, u32[]{:S(2)}) %all-to-all-start.3) | async-done | bytes 262176 | tf_op jit(solution)/shard_map/all_to_all | solution.py:351
  116.8 2.4 %shard_map.101 = (f32[4,8,1920]{2,1,0:T(8,128)}, f32[4,8,1920]{2,1,0:T(8,128)}) custom-call(f32[4,8,1920]{2,1,0:T(8,128)S(1)} %shard_map.99.base_ref, f32[512,128]{1,0:T(8,128)S(1)} %bitcast.29, f32[4,8,1920]{2,1,0:T(8,128)S(1)} %get-tuple-element.14.state_ref, bf16[4,6,8,1920]{3,2,1,0:T(8,128)(2,1)} %bitcast.39, bf16[72,256]{1,0:T(8,128)(2,1)S(1)} %bitcast.33, ...), custom_call_target="tpu_custom_call" | custom-call | tf_op jit(solution)/shard_map/pallas_call | solution.py:341
  (9 shorter events, 0.2 us)
Async XLA Ops:
  2.8 33.6 %all-to-all-start = ((f32[16,32,128]{2,1,0:T(8,128)}), f32[16,32,128]{2,1,0:T(8,128)S(1)}, u32[]{:S(2)}, u32[]{:S(2)}) async-start(f32[16,32,128]{2,1,0:T(8,128)} %bitcast.9), calls=%async_computation | async-start | bytes 524288 | tf_op jit(solution)/shard_map/all_to_all | solution.py:351
  18.0 43.4 %copy-start.1 = (f32[1,4,8,1920]{3,2,1,0:T(8,128)S(1)}, f32[1,4,8,1920]{3,2,1,0:T(8,128)}, u32[]{:S(2)}) copy-start(f32[1,4,8,1920]{3,2,1,0:T(8,128)} %param.9) | copy-start | bytes 737284
  18.1 43.4 %copy-start.4 = (bf16[1,72,256]{2,1,0:T(8,128)(2,1)S(1)}, bf16[1,72,256]{2,1,0:T(8,128)(2,1)}, u32[]{:S(2)}) copy-start(bf16[1,72,256]{2,1,0:T(8,128)(2,1)} %param.15) | copy-start | bytes 110596
  18.1 43.4 %copy-start.7 = (s32[2,256]{1,0:T(2,128)S(1)}, s32[2,256]{1,0:T(2,128)}, u32[]{:S(2)}) copy-start(s32[2,256]{1,0:T(2,128)} %src_ref.3) | copy-start | bytes 6148
  18.1 43.4 %copy-start.8 = (s32[2,256]{1,0:T(2,128)S(1)}, s32[2,256]{1,0:T(2,128)}, u32[]{:S(2)}) copy-start(s32[2,256]{1,0:T(2,128)} %dst_ref.3) | copy-start | bytes 6148
  18.1 25.0 %collective-permute-start = (f32[4,1920]{1,0:T(4,128)S(1)}, f32[4,1920]{1,0:T(4,128)S(1)}, u32[]{:S(2)}, u32[]{:S(2)}) collective-permute-start(f32[4,1920]{1,0:T(4,128)S(1)} %get-tuple-element.11), channel_id=1, source_target_pairs={{0,1},{1,2},{2,3},{3,0},{4,5},{5,6},{6,7},{7,4},{8,9},{9,10},{10,1... | collective-permute-start | bytes 92168 | tf_op jit(solution)/shard_map/ppermute | solution.py:356
  20.2 22.9 %collective-permute-start.1 = (f32[4,1920]{1,0:T(4,128)S(1)}, f32[4,1920]{1,0:T(4,128)S(1)}, u32[]{:S(2)}, u32[]{:S(2)}) collective-permute-start(f32[4,1920]{1,0:T(4,128)S(1)} %get-tuple-element.12), channel_id=1, source_target_pairs={{0,3},{1,0},{2,1},{3,2},{4,7},{5,4},{6,5},{7,6},{8,11},{9,8},{10,9... | collective-permute-start | bytes 92168 | tf_op jit(solution)/shard_map/ppermute | solution.py:357
  37.3 24.2 %all-to-all-start.1 = ((f32[16,32,128]{2,1,0:T(8,128)}), f32[16,32,128]{2,1,0:T(8,128)S(1)}, u32[]{:S(2)}, u32[]{:S(2)}) async-start(f32[16,32,128]{2,1,0:T(8,128)} %shard_map.97), calls=%async_computation.1 | async-start | bytes 524288 | tf_op jit(solution)/shard_map/all_to_all | solution.py:351
  43.1 7.7 %collective-permute-start.2 = (f32[10,1920]{1,0:T(8,128)S(1)}, f32[10,1920]{1,0:T(8,128)S(1)}, u32[]{:S(2)}, u32[]{:S(2)}) collective-permute-start(f32[10,1920]{1,0:T(8,128)S(1)} %pad_maximum_fusion), channel_id=1, source_target_pairs={{0,4},{4,8},{8,12},{12,16},{16,20},{20,24},{24,28},{1,5},{5,9},{9,... | collective-permute-start | bytes 230408 | tf_op jit(solution)/shard_map/ppermute | solution.py:361
  46.4 7.1 %collective-permute-start.3 = (f32[10,1920]{1,0:T(8,128)S(1)}, f32[10,1920]{1,0:T(8,128)S(1)}, u32[]{:S(2)}, u32[]{:S(2)}) collective-permute-start(f32[10,1920]{1,0:T(8,128)S(1)} %pad_maximum_fusion.1), channel_id=1, source_target_pairs={{4,0},{8,4},{12,8},{16,12},{20,16},{24,20},{28,24},{5,1},{9,5},{13... | collective-permute-start | bytes 230408 | tf_op jit(solution)/shard_map/ppermute | solution.py:362
  53.4 0.9 copy-start
  54.4 0.9 copy-start.2
  55.3 0.7 copy-start.5
  56.0 52.4 %copy-start.3 = (f32[1,4,8,1920]{3,2,1,0:T(8,128)S(1)}, f32[1,4,8,1920]{3,2,1,0:T(8,128)}, u32[]{:S(2)}) copy-start(f32[1,4,8,1920]{3,2,1,0:T(8,128)} %param.8) | copy-start | bytes 737284
  56.0 52.4 %copy-start.6 = (s32[4,8,4]{1,2,0:T(4,128)S(1)}, s32[4,8,4]{1,2,0:T(4,128)}, u32[]{:S(2)}) copy-start(s32[4,8,4]{1,2,0:T(4,128)} %param.11) | copy-start | bytes 1540
  64.4 28.1 %all-to-all-start.2 = ((f32[16,32,128]{2,1,0:T(8,128)}), f32[16,32,128]{2,1,0:T(8,128)S(1)}, u32[]{:S(2)}, u32[]{:S(2)}) async-start(f32[16,32,128]{2,1,0:T(8,128)} %bitcast.16), calls=%async_computation.2 | async-start | bytes 524288 | tf_op jit(solution)/shard_map/all_to_all | solution.py:351
  74.7 24.2 %collective-permute-start.4 = (f32[4,1920]{1,0:T(4,128)S(1)}, f32[4,1920]{1,0:T(4,128)S(1)}, u32[]{:S(2)}, u32[]{:S(2)}) collective-permute-start(f32[4,1920]{1,0:T(4,128)S(1)} %get-tuple-element.15), channel_id=1, source_target_pairs={{0,1},{1,2},{2,3},{3,0},{4,5},{5,6},{6,7},{7,4},{8,9},{9,10},{10,1... | collective-permute-start | bytes 92168 | tf_op jit(solution)/shard_map/ppermute | solution.py:356
  76.6 22.3 %collective-permute-start.5 = (f32[4,1920]{1,0:T(4,128)S(1)}, f32[4,1920]{1,0:T(4,128)S(1)}, u32[]{:S(2)}, u32[]{:S(2)}) collective-permute-start(f32[4,1920]{1,0:T(4,128)S(1)} %get-tuple-element.16), channel_id=1, source_target_pairs={{0,3},{1,0},{2,1},{3,2},{4,7},{5,4},{6,5},{7,6},{8,11},{9,8},{10,9... | collective-permute-start | bytes 92168 | tf_op jit(solution)/shard_map/ppermute | solution.py:357
  93.3 23.5 %all-to-all-start.3 = ((f32[16,32,128]{2,1,0:T(8,128)}), f32[16,32,128]{2,1,0:T(8,128)S(1)}, u32[]{:S(2)}, u32[]{:S(2)}) async-start(f32[16,32,128]{2,1,0:T(8,128)} %shard_map.100), calls=%async_computation.3 | async-start | bytes 524288 | tf_op jit(solution)/shard_map/all_to_all | solution.py:351
  99.0 7.8 %collective-permute-start.6 = (f32[10,1920]{1,0:T(8,128)S(1)}, f32[10,1920]{1,0:T(8,128)S(1)}, u32[]{:S(2)}, u32[]{:S(2)}) collective-permute-start(f32[10,1920]{1,0:T(8,128)S(1)} %pad_maximum_fusion.2), channel_id=1, source_target_pairs={{0,4},{4,8},{8,12},{12,16},{16,20},{20,24},{24,28},{1,5},{5,9},{9,... | collective-permute-start | bytes 230408 | tf_op jit(solution)/shard_map/ppermute | solution.py:361
  100.9 7.5 %collective-permute-start.7 = (f32[10,1920]{1,0:T(8,128)S(1)}, f32[10,1920]{1,0:T(8,128)S(1)}, u32[]{:S(2)}, u32[]{:S(2)}) collective-permute-start(f32[10,1920]{1,0:T(8,128)S(1)} %pad_maximum_fusion.3), channel_id=1, source_target_pairs={{4,0},{8,4},{12,8},{16,12},{20,16},{24,20},{28,24},{5,1},{9,5},{13... | collective-permute-start | bytes 230408 | tf_op jit(solution)/shard_map/ppermute | solution.py:362

commit v2 on v1

--- a/solution.py
+++ b/solution.py
@@ -157,20 +157,31 @@
 
 
 def tile_kernel(
-    cols_ref, tiles_hbm, state_ref, left_ref, right_ref, below_ref, above_ref, source_ref, out_ref, tiles_ref, wide, chosen, partial, sems
+    cols_hbm, tiles_hbm, state_ref, left_ref, right_ref, below_ref, above_ref, source_hbm, out_ref, cols_ref, tiles_ref, source_ref, wide, chosen, partial, sems, tile_sems
 ):
     def fetch(p):
-        return pltpu.make_async_copy(tiles_hbm.at[p], tiles_ref.at[p], sems.at[p])
-
+        return pltpu.make_async_copy(tiles_hbm.at[p], tiles_ref.at[p], tile_sems.at[p])
+
+    copies = [pltpu.make_async_copy(cols_hbm, cols_ref, sems.at[0])]
+    for row in range(SB):
+        base = (row + 1) * 16
+        copies.append(
+            pltpu.make_async_copy(state_ref.at[row], wide.at[pl.ds(base, CB)], sems.at[row + 1])
+        )
+    late = pltpu.make_async_copy(source_hbm, source_ref, sems.at[SB + 1])
+    for copy in copies:
+        copy.start()
     for p in range(SB):
         fetch(p).start()
-    wide[0:10, :] = below_ref[...]
-    wide[(SB + 1) * 16 : (SB + 1) * 16 + 10, :] = above_ref[...]
-    for row in range(SB):
-        base = (row + 1) * 16
-        wide[base : base + 8, :] = state_ref[row]
+    late.start()
+    wide[0:CB, :] = below_ref[...]
+    wide[(SB + 1) * 16 : (SB + 1) * 16 + CB, :] = above_ref[...]
+    for row, base in enumerate([16, 32, 48, 64, 0, (SB + 1) * 16]):
         wide[base + 8 : base + 9, :] = left_ref[row : row + 1, :]
         wide[base + 9 : base + 10, :] = right_ref[row : row + 1, :]
+    for copy in copies:
+        copy.wait()
+    late.wait()
 
     def block_row(p, carry):
         fetch(p).wait()
@@ -201,9 +212,7 @@
     lax.fori_loop(0, SB, block_row, 0)
 
 
-def finish(base_ref, spectral_ref, state_ref, inverse_hbm, coef_ref, dst_ref, residual_ref, next_ref, lagged, inverse_ref, sem):
-    fetch = pltpu.make_async_copy(inverse_hbm, inverse_ref, sem)
-    fetch.start()
+def finish(base_ref, spectral_ref, state_ref, inverse_ref, coef_ref, dst_ref, residual_ref, next_ref, lagged):
     coef = coef_ref[...].astype(jnp.float32)
     spread, cells = [], []
     for side in range(2):
@@ -228,7 +237,6 @@
     )
     count = SB * CB * 8
     put(lagged, 0, count, placed[:count] + (placed[count : 2 * count] + placed[2 * count :]))
-    fetch.wait()
     for p in range(SB):
         first = p * STRIPS * 8
         spectral = jnp.concatenate(
@@ -248,17 +256,17 @@
 
 
 def middle_kernel(
-    base_ref, spectral_ref, state_ref, inverse_hbm, coef_ref, dst_ref, src_ref, next_ref, send_ref, low_ref, high_ref, residual_ref, lagged, inverse, sem
+    base_ref, spectral_ref, state_ref, inverse_ref, coef_ref, dst_ref, src_ref, next_ref, send_ref, low_ref, high_ref, residual_ref, lagged
 ):
-    finish(base_ref, spectral_ref, state_ref, inverse_hbm, coef_ref, dst_ref, residual_ref, next_ref, lagged, inverse, sem)
+    finish(base_ref, spectral_ref, state_ref, inverse_ref, coef_ref, dst_ref, residual_ref, next_ref, lagged)
     emit_exchange(next_ref, src_ref, send_ref)
     emit_edges(next_ref, low_ref, high_ref)
 
 
 def last_kernel(
-    base_ref, spectral_ref, state_ref, inverse_hbm, coef_ref, dst_ref, next_ref, residual_ref, lagged, inverse, sem
+    base_ref, spectral_ref, state_ref, inverse_ref, coef_ref, dst_ref, next_ref, residual_ref, lagged
 ):
-    finish(base_ref, spectral_ref, state_ref, inverse_hbm, coef_ref, dst_ref, residual_ref, next_ref, lagged, inverse, sem)
+    finish(base_ref, spectral_ref, state_ref, inverse_ref, coef_ref, dst_ref, residual_ref, next_ref, lagged)
 
 
 def f32(*shape):
@@ -270,8 +278,6 @@
 SEND = f32(NT * SHARE, LANES)
 FINISH_SCRATCH = [
     pltpu.VMEM((3, SB * CB * 8, LANES), jnp.float32),
-    pltpu.VMEM((SB, NV, CB, WIDTH), jnp.bfloat16),
-    pltpu.SemaphoreType.DMA,
 ]
 def room(mebibytes):
     return pltpu.CompilerParams(vmem_limit_bytes=mebibytes << 20)
@@ -305,26 +311,27 @@
 
 
 def tile_call(cols, tiles, state, left, right, below, above, source):
-    in_vmem = pl.BlockSpec(memory_space=pltpu.VMEM)
+    in_vmem, raw = pl.BlockSpec(memory_space=pltpu.VMEM), pl.BlockSpec(memory_space=pl.ANY)
     return pl.pallas_call(
         tile_kernel,
         out_shape=STATE,
-        in_specs=[pl.BlockSpec(memory_space=pltpu.SMEM), pl.BlockSpec(memory_space=pltpu.HBM)] + [in_vmem] * 6,
+        in_specs=[raw] * 3 + [in_vmem] * 4 + [raw],
         scratch_shapes=[
+            pltpu.SMEM(cols.shape, cols.dtype),
             pltpu.VMEM(tiles.shape, tiles.dtype),
+            pltpu.VMEM(source.shape, source.dtype),
             pltpu.VMEM(((SB + 2) * 16, WIDTH), jnp.float32),
             pltpu.VMEM((CB * 8, WIDTH), jnp.float32),
             pltpu.VMEM((2 * BLK // LANES, NV * CB * K, LANES), jnp.float32),
+            pltpu.SemaphoreType.DMA((SB + 2,)),
             pltpu.SemaphoreType.DMA((SB,)),
         ],
         compiler_params=room(8),
-    )(cols, in_hbm(tiles), state, left, right, below, above, source)
+    )(in_hbm(cols), in_hbm(tiles), state, left, right, below, above, in_hbm(source))
 
 
 def finish_specs(count):
-    specs = [pl.BlockSpec(memory_space=pltpu.VMEM)] * count
-    specs[3] = pl.BlockSpec(memory_space=pltpu.HBM)
-    return specs
+    return [pl.BlockSpec(memory_space=pltpu.VMEM)] * count
 
 
 def middle_call(base, spectral, state, inverse, coef, dst, src):
@@ -334,7 +341,7 @@
         in_specs=finish_specs(7),
         scratch_shapes=[pltpu.VMEM((SB, CB, WIDTH), jnp.float32)] + FINISH_SCRATCH,
         compiler_params=room(8),
-    )(base, spectral, state, in_hbm(inverse), coef, dst, src)
+    )(base, spectral, state, inverse, coef, dst, src)
 
 
 def last_call(base, spectral, state, inverse, coef, dst):
@@ -344,7 +351,7 @@
         in_specs=finish_specs(6),
         scratch_shapes=FINISH_SCRATCH,
         compiler_params=room(8),
-    )(base, spectral, state, in_hbm(inverse), coef, dst)
+    )(base, spectral, state, inverse, coef, dst)
 
 
 def exchange(array):
@@ -352,14 +359,14 @@
 
 
 def halos(state, low_edge, high_edge):
+    n = lax.axis_size("span")
+    below = lax.ppermute(state[SB - 1], "span", [(i, i + 1) for i in range(n - 1)])
+    above = lax.ppermute(state[0], "span", [(i + 1, i) for i in range(n - 1)])
+    low_edge = jnp.concatenate([low_edge, below[CB - 1 :], above[CB - 1 :]], axis=0)
+    high_edge = jnp.concatenate([high_edge, below[:1], above[:1]], axis=0)
     n = lax.axis_size("chord")
     left = lax.ppermute(low_edge, "chord", [(i, (i + 1) % n) for i in range(n)])
     right = lax.ppermute(high_edge, "chord", [(i, (i - 1) % n) for i in range(n)])
-    n = lax.axis_size("span")
-    last = jnp.concatenate([state[SB - 1], left[SB - 1 :], right[SB - 1 :]], axis=0)
-    first = jnp.concatenate([state[0], left[:1], right[:1]], axis=0)
-    below = lax.ppermute(last, "span", [(i, i + 1) for i in range(n - 1)])
-    above = lax.ppermute(first, "span", [(i + 1, i) for i in range(n - 1)])
     return left, right, below, above
 
 
@@ -375,7 +382,7 @@
         received = exchange(send.reshape(NT, SHARE, LANES))
         left, right, below, above = halos(state, low_edge, high_edge)
         spectral = exchange(spectral_call(who, received)).reshape(NT * SHARE, LANES)
-        base = tile_call(tile_cols, tiles, state, left, right, below, above, source)
+        base = tile_call(tile_cols, tiles, in_hbm(state) if sweep == 0 else state, left, right, below, above, source)
         if sweep < SWEEPS - 1:
             state, send, low_edge, high_edge = middle_call(
                 base, spectral, state, inverse, coef, face_dst, face_src

time: 120 us -> 115 us (0.958)
  the two profiles are of different devices: /device:TPU:22 before, /device:TPU:52 now
where the time goes in v2:
time: 115 us; the launch traced here: 114 us
  starting transfers between devices  59.3 us (52%)
  waiting for transfers between devices  37.1 us (32%)
  Pallas kernels  15.6 us (14%)
    all_to_all x4, starting transfers between devices, exchange(): return lax.all_to_all(array, 'inst', 0, 0, tiled=True)  34.4 us
    all_to_all x4, waiting for transfers between devices, exchange(): return lax.all_to_all(array, 'inst', 0, 0, tiled=True)  30.6 us
    pallas_call x2, Pallas kernels, tile_call(): pl.pallas_call(tile_kernel, out_shape=STATE, in_specs=[raw] * 3 + [in_vme...  7.82 us
    ppermute x2, starting transfers between devices, halos(): lax.ppermute(high_edge, 'chord', [(i, (i - 1) % n) for i in range(n)])  7.07 us
    ppermute x2, starting transfers between devices, halos(): above = lax.ppermute(state[0], 'span', [(i + 1, i) for i in range(n - 1)])  7.07 us
    ppermute x2, starting transfers between devices, halos(): lax.ppermute(state[SB - 1], 'span', [(i, i + 1) for i in range(n - 1)])  6.42 us
    ppermute x2, waiting for transfers between devices, halos(): left = lax.ppermute(low_edge, 'chord', [(i, (i + 1) % n) for i in range(n)])  4.62 us
    ppermute x2, starting transfers between devices, halos(): left = lax.ppermute(low_edge, 'chord', [(i, (i + 1) % n) for i in range(n)])  4.33 us
  transfers between devices with their start and end apart: 12, of which 6 were waited for; matrix products, arithmetic and copies ran while one was open for 1% of the time, Pallas kernels for 8%

profile of v2, /device:TPU:52, one launch (start us, length us, event | category | flops | bytes accessed | tf_op | source)
XLA Modules:
  0.0 113.9 jit_solution(14474458769953073387)
XLA Ops:
  0.6 2.2 %shard_map.95 = (f32[512,128]{1,0:T(8,128)}, f32[4,1920]{1,0:T(4,128)S(1)}, f32[4,1920]{1,0:T(4,128)S(1)}) custom-call(f32[4,8,1920]{2,1,0:T(8,128)} %bitcast.25, s32[2,256]{1,0:T(2,128)} %src_ref.3), custom_call_target="tpu_custom_call" | custom-call | tf_op jit(solution)/shard_map/pallas_call | solution.py:291
  2.8 0.0 copy-start
  2.9 0.0 copy-start.1
  2.9 0.0 copy-start.2
  2.9 0.0 copy-start.3
  2.9 0.0 copy-start.4
  2.9 15.4 %all-to-all-start = ((f32[16,32,128]{2,1,0:T(8,128)}), f32[16,32,128]{2,1,0:T(8,128)S(1)}, u32[]{:S(2)}, u32[]{:S(2)}) async-start(f32[16,32,128]{2,1,0:T(8,128)} %bitcast.9), calls=%async_computation | async-start | bytes 524288 | tf_op jit(solution)/shard_map/all_to_all | solution.py:358
  18.3 0.9 slice_bitcast_fusion.3
  19.1 3.2 %collective-permute-start = (f32[8,1920]{1,0:T(8,128)S(1)}, f32[8,1920]{1,0:T(8,128)S(1)}, u32[]{:S(2)}, u32[]{:S(2)}) collective-permute-start(f32[8,1920]{1,0:T(8,128)S(1)} %get-tuple-element.22), channel_id=1, source_target_pairs={{0,4},{4,8},{8,12},{12,16},{16,20},{20,24},{24,28},{1,5},{5,9},{9,... | collective-permute-start | bytes 184328 | tf_op jit(solution)/shard_map/ppermute | solution.py:363
  22.3 3.6 %collective-permute-start.1 = (f32[8,1920]{1,0:T(8,128)S(1)}, f32[8,1920]{1,0:T(8,128)S(1)}, u32[]{:S(2)}, u32[]{:S(2)}) collective-permute-start(f32[8,1920]{1,0:T(8,128)S(1)} %get-tuple-element.23), channel_id=1, source_target_pairs={{4,0},{8,4},{12,8},{16,12},{20,16},{24,20},{28,24},{5,1},{9,5},{13... | collective-permute-start | bytes 184328 | tf_op jit(solution)/shard_map/ppermute | solution.py:364
  25.9 10.3 %all-to-all-done.in_ref = f32[16,32,128]{2,1,0:T(8,128)S(1)} async-done(((f32[16,32,128]{2,1,0:T(8,128)}), f32[16,32,128]{2,1,0:T(8,128)S(1)}, u32[]{:S(2)}, u32[]{:S(2)}) %all-to-all-start) | async-done | bytes 262176 | tf_op jit(solution)/shard_map/all_to_all | solution.py:358
  36.2 0.9 shard_map.97
  37.0 6.3 %all-to-all-start.1 = ((f32[16,32,128]{2,1,0:T(8,128)}), f32[16,32,128]{2,1,0:T(8,128)S(1)}, u32[]{:S(2)}, u32[]{:S(2)}) async-start(f32[16,32,128]{2,1,0:T(8,128)} %shard_map.97), calls=%async_computation.1 | async-start | bytes 524288 | tf_op jit(solution)/shard_map/all_to_all | solution.py:358
  43.3 0.0 collective-permute-done.below_ref
  43.3 0.0 collective-permute-done.1.above_ref
  43.4 1.9 %collective-permute-start.3 = (f32[6,1920]{1,0:T(8,128)S(1)}, f32[6,1920]{1,0:T(8,128)S(1)}, u32[]{:S(2)}, u32[]{:S(2)}) collective-permute-start(f32[6,1920]{1,0:T(8,128)S(1)} %pad_maximum_fusion.1), channel_id=1, source_target_pairs={{0,3},{1,0},{2,1},{3,2},{4,7},{5,4},{6,5},{7,6},{8,11},{9,8},{10,9... | collective-permute-start | bytes 138248 | tf_op jit(solution)/shard_map/ppermute | solution.py:369
  45.3 2.4 %collective-permute-start.2 = (f32[6,1920]{1,0:T(8,128)S(1)}, f32[6,1920]{1,0:T(8,128)S(1)}, u32[]{:S(2)}, u32[]{:S(2)}) collective-permute-start(f32[6,1920]{1,0:T(8,128)S(1)} %pad_maximum_fusion), channel_id=1, source_target_pairs={{0,1},{1,2},{2,3},{3,0},{4,5},{5,6},{6,7},{7,4},{8,9},{9,10},{10,1... | collective-permute-start | bytes 138248 | tf_op jit(solution)/shard_map/ppermute | solution.py:368
  47.7 0.0 collective-permute-done.3.right_ref
  47.7 4.6 %collective-permute-done.2.left_ref = f32[6,1920]{1,0:T(8,128)S(1)} collective-permute-done((f32[6,1920]{1,0:T(8,128)S(1)}, f32[6,1920]{1,0:T(8,128)S(1)}, u32[]{:S(2)}, u32[]{:S(2)}) %collective-permute-start.2) | collective-permute-done | bytes 46112 | tf_op jit(solution)/shard_map/ppermute | solution.py:368
  52.4 3.8 %shard_map.96.base_ref = f32[4,8,1920]{2,1,0:T(8,128)S(1)} custom-call(s32[4,4,8]{2,1,0:T(4,128)} %bitcast.38, bf16[4,8,6,4,1920]{4,3,2,1,0:T(4,128)(2,1)} %bitcast.34, f32[4,8,1920]{2,1,0:T(8,128)} %bitcast.26, f32[6,1920]{1,0:T(8,128)S(1)} %collective-permute-done.2.left_ref, f32[6,1920]{1,0:T(8,128)S(1)} %collective-permute-done.3.right_ref, ...), custom_call_target="tpu_custom_call" | custom-call | tf_op jit(solution)/shard_map/pallas_call | solution.py:315
  56.2 4.6 %all-to-all-done.1 = f32[16,32,128]{2,1,0:T(8,128)S(1)} async-done(((f32[16,32,128]{2,1,0:T(8,128)}), f32[16,32,128]{2,1,0:T(8,128)S(1)}, u32[]{:S(2)}, u32[]{:S(2)}) %all-to-all-start.1) | async-done | bytes 262176 | tf_op jit(solution)/shard_map/all_to_all | solution.py:358
  60.8 0.0 copy-done
  60.8 0.0 copy-done.1
  60.8 0.0 copy-done.2
  60.8 0.0 copy-done.3
  60.8 0.0 copy-done.4
  60.8 2.2 %shard_map.98 = (f32[4,8,1920]{2,1,0:T(8,128)S(1)}, f32[512,128]{1,0:T(8,128)}, f32[4,1920]{1,0:T(4,128)S(1)}, f32[4,1920]{1,0:T(4,128)S(1)}) custom-call(f32[4,8,1920]{2,1,0:T(8,128)S(1)} %shard_map.96.base_ref, f32[512,128]{1,0:T(8,128)S(1)} %bitcast.30, f32[4,8,1920]{2,1,0:T(8,128)S(1)} %bitcast.27, bf16[4,6,8,1920]{3,2,1,0:T(8,128)(2,1)S(1)} %bitcast.28, ...), custom_call_target="tpu_custom_call" | custom-call | tf_op jit(solution)/shard_map/pallas_call | solution.py:338
  63.0 7.5 %all-to-all-start.2 = ((f32[16,32,128]{2,1,0:T(8,128)}), f32[16,32,128]{2,1,0:T(8,128)S(1)}, u32[]{:S(2)}, u32[]{:S(2)}) async-start(f32[16,32,128]{2,1,0:T(8,128)} %bitcast.16), calls=%async_computation.2 | async-start | bytes 524288 | tf_op jit(solution)/shard_map/all_to_all | solution.py:358
  70.5 3.2 %collective-permute-start.4 = (f32[8,1920]{1,0:T(8,128)S(1)}, f32[8,1920]{1,0:T(8,128)S(1)}, u32[]{:S(2)}, u32[]{:S(2)}) collective-permute-start(f32[8,1920]{1,0:T(8,128)S(1)} %get-tuple-element.20), channel_id=1, source_target_pairs={{0,4},{4,8},{8,12},{12,16},{16,20},{20,24},{24,28},{1,5},{5,9},{9,... | collective-permute-start | bytes 184328 | tf_op jit(solution)/shard_map/ppermute | solution.py:363
  73.7 3.5 %collective-permute-start.5 = (f32[8,1920]{1,0:T(8,128)S(1)}, f32[8,1920]{1,0:T(8,128)S(1)}, u32[]{:S(2)}, u32[]{:S(2)}) collective-permute-start(f32[8,1920]{1,0:T(8,128)S(1)} %get-tuple-element.21), channel_id=1, source_target_pairs={{4,0},{8,4},{12,8},{16,12},{20,16},{24,20},{28,24},{5,1},{9,5},{13... | collective-permute-start | bytes 184328 | tf_op jit(solution)/shard_map/ppermute | solution.py:364
  77.3 11.0 %all-to-all-done.2.in_ref = f32[16,32,128]{2,1,0:T(8,128)S(1)} async-done(((f32[16,32,128]{2,1,0:T(8,128)}), f32[16,32,128]{2,1,0:T(8,128)S(1)}, u32[]{:S(2)}, u32[]{:S(2)}) %all-to-all-start.2) | async-done | bytes 262176 | tf_op jit(solution)/shard_map/all_to_all | solution.py:358
  88.3 0.9 shard_map.100
  89.2 5.4 %all-to-all-start.3 = ((f32[16,32,128]{2,1,0:T(8,128)}), f32[16,32,128]{2,1,0:T(8,128)S(1)}, u32[]{:S(2)}, u32[]{:S(2)}) async-start(f32[16,32,128]{2,1,0:T(8,128)} %shard_map.100), calls=%async_computation.3 | async-start | bytes 524288 | tf_op jit(solution)/shard_map/all_to_all | solution.py:358
  94.5 0.0 collective-permute-done.4.below_ref
  94.6 0.0 collective-permute-done.5.above_ref
  94.6 1.9 %collective-permute-start.6 = (f32[6,1920]{1,0:T(8,128)S(1)}, f32[6,1920]{1,0:T(8,128)S(1)}, u32[]{:S(2)}, u32[]{:S(2)}) collective-permute-start(f32[6,1920]{1,0:T(8,128)S(1)} %pad_maximum_fusion.2), channel_id=1, source_target_pairs={{0,1},{1,2},{2,3},{3,0},{4,5},{5,6},{6,7},{7,4},{8,9},{9,10},{10,1... | collective-permute-start | bytes 138248 | tf_op jit(solution)/shard_map/ppermute | solution.py:368
  96.6 5.1 %collective-permute-start.7 = (f32[6,1920]{1,0:T(8,128)S(1)}, f32[6,1920]{1,0:T(8,128)S(1)}, u32[]{:S(2)}, u32[]{:S(2)}) collective-permute-start(f32[6,1920]{1,0:T(8,128)S(1)} %pad_maximum_fusion.3), channel_id=1, source_target_pairs={{0,3},{1,0},{2,1},{3,2},{4,7},{5,4},{6,5},{7,6},{8,11},{9,8},{10,9... | collective-permute-start | bytes 138248 | tf_op jit(solution)/shard_map/ppermute | solution.py:369
  101.7 0.0 collective-permute-done.6.left_ref
  101.8 1.8 %collective-permute-done.7.right_ref = f32[6,1920]{1,0:T(8,128)S(1)} collective-permute-done((f32[6,1920]{1,0:T(8,128)S(1)}, f32[6,1920]{1,0:T(8,128)S(1)}, u32[]{:S(2)}, u32[]{:S(2)}) %collective-permute-start.7) | collective-permute-done | bytes 46112 | tf_op jit(solution)/shard_map/ppermute | solution.py:369
  103.6 4.0 %shard_map.99.base_ref = f32[4,8,1920]{2,1,0:T(8,128)S(1)} custom-call(s32[4,4,8]{2,1,0:T(4,128)} %bitcast.39, bf16[4,8,6,4,1920]{4,3,2,1,0:T(4,128)(2,1)} %bitcast.35, f32[4,8,1920]{2,1,0:T(8,128)S(1)} %get-tuple-element.14.state_ref, f32[6,1920]{1,0:T(8,128)S(1)} %collective-permute-done.6.left_ref, f32[6,1920]{1,0:T(8,128)S(1)} %collective-permute-done.7.right_ref, ...), custom_call_target="tpu_custom_call" | custom-call | tf_op jit(solution)/shard_map/pallas_call | solution.py:315
  107.6 4.7 %all-to-all-done.3 = f32[16,32,128]{2,1,0:T(8,128)S(1)} async-done(((f32[16,32,128]{2,1,0:T(8,128)}), f32[16,32,128]{2,1,0:T(8,128)S(1)}, u32[]{:S(2)}, u32[]{:S(2)}) %all-to-all-start.3) | async-done | bytes 262176 | tf_op jit(solution)/shard_map/all_to_all | solution.py:358
  112.3 1.6 %shard_map.101 = (f32[4,8,1920]{2,1,0:T(8,128)}, f32[4,8,1920]{2,1,0:T(8,128)}) custom-call(f32[4,8,1920]{2,1,0:T(8,128)S(1)} %shard_map.99.base_ref, f32[512,128]{1,0:T(8,128)S(1)} %bitcast.31, f32[4,8,1920]{2,1,0:T(8,128)S(1)} %get-tuple-element.14.state_ref, bf16[4,6,8,1920]{3,2,1,0:T(8,128)(2,1)S(1)} %bitcast.29, bf16[72,256]{1,0:T(8,128)(2,1)S(1)} %bitcast.33, ...), custom_call_target="tpu_custom_call" | custom-call | tf_op jit(solution)/shard_map/pallas_call | solution.py:348
  (9 shorter events, 0.2 us)
Async XLA Ops:
  2.8 58.0 %copy-start = (f32[1,4,8,1920]{3,2,1,0:T(8,128)S(1)}, f32[1,4,8,1920]{3,2,1,0:T(8,128)}, u32[]{:S(2)}) copy-start(f32[1,4,8,1920]{3,2,1,0:T(8,128)} %param.9) | copy-start | bytes 737284
  2.9 58.0 %copy-start.1 = (bf16[1,4,8,6,1920]{4,2,3,1,0:T(8,128)(2,1)S(1)}, bf16[1,4,8,6,1920]{4,2,3,1,0:T(8,128)(2,1)}, u32[]{:S(2)}) copy-start(bf16[1,4,8,6,1920]{4,2,3,1,0:T(8,128)(2,1)} %param.12) | copy-start | bytes 2211844
  2.9 57.9 %copy-start.2 = (bf16[1,72,256]{2,1,0:T(8,128)(2,1)S(1)}, bf16[1,72,256]{2,1,0:T(8,128)(2,1)}, u32[]{:S(2)}) copy-start(bf16[1,72,256]{2,1,0:T(8,128)(2,1)} %param.15) | copy-start | bytes 110596
  2.9 57.9 %copy-start.3 = (s32[2,256]{1,0:T(2,128)S(1)}, s32[2,256]{1,0:T(2,128)}, u32[]{:S(2)}) copy-start(s32[2,256]{1,0:T(2,128)} %src_ref.3) | copy-start | bytes 6148
  2.9 57.9 %copy-start.4 = (s32[2,256]{1,0:T(2,128)S(1)}, s32[2,256]{1,0:T(2,128)}, u32[]{:S(2)}) copy-start(s32[2,256]{1,0:T(2,128)} %dst_ref.3) | copy-start | bytes 6148
  2.9 33.3 %all-to-all-start = ((f32[16,32,128]{2,1,0:T(8,128)}), f32[16,32,128]{2,1,0:T(8,128)S(1)}, u32[]{:S(2)}, u32[]{:S(2)}) async-start(f32[16,32,128]{2,1,0:T(8,128)} %bitcast.9), calls=%async_computation | async-start | bytes 524288 | tf_op jit(solution)/shard_map/all_to_all | solution.py:358
  19.1 24.1 %collective-permute-start = (f32[8,1920]{1,0:T(8,128)S(1)}, f32[8,1920]{1,0:T(8,128)S(1)}, u32[]{:S(2)}, u32[]{:S(2)}) collective-permute-start(f32[8,1920]{1,0:T(8,128)S(1)} %get-tuple-element.22), channel_id=1, source_target_pairs={{0,4},{4,8},{8,12},{12,16},{16,20},{20,24},{24,28},{1,5},{5,9},{9,... | collective-permute-start | bytes 184328 | tf_op jit(solution)/shard_map/ppermute | solution.py:363
  22.3 21.0 %collective-permute-start.1 = (f32[8,1920]{1,0:T(8,128)S(1)}, f32[8,1920]{1,0:T(8,128)S(1)}, u32[]{:S(2)}, u32[]{:S(2)}) collective-permute-start(f32[8,1920]{1,0:T(8,128)S(1)} %get-tuple-element.23), channel_id=1, source_target_pairs={{4,0},{8,4},{12,8},{16,12},{20,16},{24,20},{28,24},{5,1},{9,5},{13... | collective-permute-start | bytes 184328 | tf_op jit(solution)/shard_map/ppermute | solution.py:364
  37.0 23.8 %all-to-all-start.1 = ((f32[16,32,128]{2,1,0:T(8,128)}), f32[16,32,128]{2,1,0:T(8,128)S(1)}, u32[]{:S(2)}, u32[]{:S(2)}) async-start(f32[16,32,128]{2,1,0:T(8,128)} %shard_map.97), calls=%async_computation.1 | async-start | bytes 524288 | tf_op jit(solution)/shard_map/all_to_all | solution.py:358
  43.4 4.4 %collective-permute-start.3 = (f32[6,1920]{1,0:T(8,128)S(1)}, f32[6,1920]{1,0:T(8,128)S(1)}, u32[]{:S(2)}, u32[]{:S(2)}) collective-permute-start(f32[6,1920]{1,0:T(8,128)S(1)} %pad_maximum_fusion.1), channel_id=1, source_target_pairs={{0,3},{1,0},{2,1},{3,2},{4,7},{5,4},{6,5},{7,6},{8,11},{9,8},{10,9... | collective-permute-start | bytes 138248 | tf_op jit(solution)/shard_map/ppermute | solution.py:369
  45.3 7.0 %collective-permute-start.2 = (f32[6,1920]{1,0:T(8,128)S(1)}, f32[6,1920]{1,0:T(8,128)S(1)}, u32[]{:S(2)}, u32[]{:S(2)}) collective-permute-start(f32[6,1920]{1,0:T(8,128)S(1)} %pad_maximum_fusion), channel_id=1, source_target_pairs={{0,1},{1,2},{2,3},{3,0},{4,5},{5,6},{6,7},{7,4},{8,9},{9,10},{10,1... | collective-permute-start | bytes 138248 | tf_op jit(solution)/shard_map/ppermute | solution.py:368
  63.0 25.3 %all-to-all-start.2 = ((f32[16,32,128]{2,1,0:T(8,128)}), f32[16,32,128]{2,1,0:T(8,128)S(1)}, u32[]{:S(2)}, u32[]{:S(2)}) async-start(f32[16,32,128]{2,1,0:T(8,128)} %bitcast.16), calls=%async_computation.2 | async-start | bytes 524288 | tf_op jit(solution)/shard_map/all_to_all | solution.py:358
  70.5 24.1 %collective-permute-start.4 = (f32[8,1920]{1,0:T(8,128)S(1)}, f32[8,1920]{1,0:T(8,128)S(1)}, u32[]{:S(2)}, u32[]{:S(2)}) collective-permute-start(f32[8,1920]{1,0:T(8,128)S(1)} %get-tuple-element.20), channel_id=1, source_target_pairs={{0,4},{4,8},{8,12},{12,16},{16,20},{20,24},{24,28},{1,5},{5,9},{9,... | collective-permute-start | bytes 184328 | tf_op jit(solution)/shard_map/ppermute | solution.py:363
  73.7 20.8 %collective-permute-start.5 = (f32[8,1920]{1,0:T(8,128)S(1)}, f32[8,1920]{1,0:T(8,128)S(1)}, u32[]{:S(2)}, u32[]{:S(2)}) collective-permute-start(f32[8,1920]{1,0:T(8,128)S(1)} %get-tuple-element.21), channel_id=1, source_target_pairs={{4,0},{8,4},{12,8},{16,12},{20,16},{24,20},{28,24},{5,1},{9,5},{13... | collective-permute-start | bytes 184328 | tf_op jit(solution)/shard_map/ppermute | solution.py:364
  89.2 23.1 %all-to-all-start.3 = ((f32[16,32,128]{2,1,0:T(8,128)}), f32[16,32,128]{2,1,0:T(8,128)S(1)}, u32[]{:S(2)}, u32[]{:S(2)}) async-start(f32[16,32,128]{2,1,0:T(8,128)} %shard_map.100), calls=%async_computation.3 | async-start | bytes 524288 | tf_op jit(solution)/shard_map/all_to_all | solution.py:358
  94.6 7.1 %collective-permute-start.6 = (f32[6,1920]{1,0:T(8,128)S(1)}, f32[6,1920]{1,0:T(8,128)S(1)}, u32[]{:S(2)}, u32[]{:S(2)}) collective-permute-start(f32[6,1920]{1,0:T(8,128)S(1)} %pad_maximum_fusion.2), channel_id=1, source_target_pairs={{0,1},{1,2},{2,3},{3,0},{4,5},{5,6},{6,7},{7,4},{8,9},{9,10},{10,1... | collective-permute-start | bytes 138248 | tf_op jit(solution)/shard_map/ppermute | solution.py:368
  96.6 7.0 %collective-permute-start.7 = (f32[6,1920]{1,0:T(8,128)S(1)}, f32[6,1920]{1,0:T(8,128)S(1)}, u32[]{:S(2)}, u32[]{:S(2)}) collective-permute-start(f32[6,1920]{1,0:T(8,128)S(1)} %pad_maximum_fusion.3), channel_id=1, source_target_pairs={{0,3},{1,0},{2,1},{3,2},{4,7},{5,4},{6,5},{7,6},{8,11},{9,8},{10,9... | collective-permute-start | bytes 138248 | tf_op jit(solution)/shard_map/ppermute | solution.py:369

commit v3 on v2

--- a/solution.py
+++ b/solution.py
@@ -21,6 +21,8 @@
 STRIPS = WIDTH // LANES
 SHARE = 32
 FACE_ROW = SB * STRIPS * 8
+OWNER = (0, 3, 6, 9, 12, 15, 2, 5, 8, 11, 14, 1, 4, 7, 10, 13)
+SLOT = tuple(OWNER.index(t) for t in range(NT))
 
 rotor_rate = 0.25
 spectral_viscosity = 0.03
@@ -112,12 +114,12 @@
     coef = spectral_coefficients()
     half = NT // 2
 
-    @pl.when(who_ref[0] != NT - 1)
+    @pl.when(who_ref[0] != OWNER[NT - 1])
     def _():
         for group in range(SHARE // 8):
             rows = slice(group * 8, group * 8 + 8)
-            sums = [in_ref[s, rows, :] + in_ref[s + half, rows, :] for s in range(half)]
-            gaps = [in_ref[s, rows, :] - in_ref[s + half, rows, :] for s in range(half)]
+            sums = [in_ref[SLOT[s], rows, :] + in_ref[SLOT[s + half], rows, :] for s in range(half)]
+            gaps = [in_ref[SLOT[s], rows, :] - in_ref[SLOT[s + half], rows, :] for s in range(half)]
             for t in range(half):
                 even = odd = None
                 for s in range(half):
@@ -126,14 +128,14 @@
                     two = gaps[s] * jnp.float32(0.5 * (near - far))
                     even = one if even is None else even + one
                     odd = two if odd is None else odd + two
-                out_ref[t, rows, :] = even + odd
-                out_ref[t + half, rows, :] = even - odd
-
-    @pl.when(who_ref[0] == NT - 1)
+                out_ref[SLOT[t], rows, :] = even + odd
+                out_ref[SLOT[t + half], rows, :] = even - odd
+
+    @pl.when(who_ref[0] == OWNER[NT - 1])
     def _():
         for t in range(NT):
-            out_ref[t, 0:16, :] = in_ref[(t - LAG) % NT, 0:16, :]
-            out_ref[t, 16:32, :] = in_ref[(t + LAG) % NT, 16:32, :]
+            out_ref[SLOT[t], 0:16, :] = in_ref[SLOT[(t - LAG) % NT], 0:16, :]
+            out_ref[SLOT[t], 16:32, :] = in_ref[SLOT[(t + LAG) % NT], 16:32, :]
 
 
 def put(ref, row, count, value):
@@ -156,11 +158,39 @@
     return product[:, :pair] + product[:, pair : 2 * pair] + product[:, 2 * pair :]
 
 
-def tile_kernel(
-    cols_hbm, tiles_hbm, state_ref, left_ref, right_ref, below_ref, above_ref, source_hbm, out_ref, cols_ref, tiles_ref, source_ref, wide, chosen, partial, sems, tile_sems
-):
+def choose(cols_ref, p, q, wide, chosen):
+    for k in range(K):
+        code = cols_ref[p, k, q]
+        a = lax.shift_right_logical(code * 11, 5)
+        side = q + code - 3 * a - 1
+        column = jnp.where(side < 0, CB, jnp.where(side == CB, CB + 1, side))
+        row = (p + a) * 16 + column
+        chosen[q * 8 + k : q * 8 + k + 1, :] = wide[pl.ds(row, 1), :]
+    return chosen[q * 8 : q * 8 + K, :]
+
+
+def weigh(tile_ref, inputs, partial, q):
+    for v in range(NV):
+        total = sum_pairs(tile_ref[v].astype(jnp.float32) * inputs)
+        for n in range(2 * BLK // LANES):
+            row = v * CB * K + q * K
+            partial[n, row : row + K, :] = total[:, n * LANES : (n + 1) * LANES]
+
+
+def sum_slots(partial, v):
+    total = None
+    for k in range(K):
+        rows = pl.ds(v * CB * K + k, CB, stride=K)
+        one = jnp.concatenate([partial[n, rows, :] for n in range(2 * BLK // LANES)], axis=1)
+        total = one if total is None else total + one
+    return fold_pair(total)
+
+
+def inner_kernel(cols_hbm, tiles_hbm, state_ref, out_ref, cols_ref, tiles_ref, wide, chosen, partial, sems, tile_sems):
     def fetch(p):
-        return pltpu.make_async_copy(tiles_hbm.at[p], tiles_ref.at[p], tile_sems.at[p])
+        return pltpu.make_async_copy(
+            tiles_hbm.at[p, pl.ds(1, CB - 2)], tiles_ref.at[p], tile_sems.at[p]
+        )
 
     copies = [pltpu.make_async_copy(cols_hbm, cols_ref, sems.at[0])]
     for row in range(SB):
@@ -168,48 +198,76 @@
         copies.append(
             pltpu.make_async_copy(state_ref.at[row], wide.at[pl.ds(base, CB)], sems.at[row + 1])
         )
-    late = pltpu.make_async_copy(source_hbm, source_ref, sems.at[SB + 1])
     for copy in copies:
         copy.start()
-    for p in range(SB):
+    for p in range(1, SB - 1):
         fetch(p).start()
-    late.start()
+    partial[...] = jnp.zeros(partial.shape, jnp.float32)
+    for copy in copies:
+        copy.wait()
+
+    def block_row(p, carry):
+        fetch(p).wait()
+        for q in range(1, CB - 1):
+            weigh(tiles_ref.at[p, q - 1], choose(cols_ref, p, q, wide, chosen), partial, q)
+        for v in range(NV):
+            out_ref[p - 1, :, v * BLK : (v + 1) * BLK] = sum_slots(partial, v)
+        return carry
+
+    lax.fori_loop(1, SB - 1, block_row, 0)
+
+
+def outer_kernel(
+    cols_hbm, tiles_hbm, state_ref, left_ref, right_ref, below_ref, above_ref, source_hbm, inner_ref, out_ref, cols_ref, rows_ref, ends_ref, source_ref, wide, chosen, partial, sems, row_sems, end_sems
+):
+    def fetch(p, slot):
+        return pltpu.make_async_copy(tiles_hbm.at[p], rows_ref.at[slot], row_sems.at[slot])
+
+    def fetch_end(n):
+        p, q = 1 + n // 2, (n % 2) * (CB - 1)
+        return pltpu.make_async_copy(tiles_hbm.at[p, q], ends_ref.at[n], end_sems.at[n])
+
+    copies = [pltpu.make_async_copy(cols_hbm, cols_ref, sems.at[0])]
+    for row in range(SB):
+        base = (row + 1) * 16
+        copies.append(
+            pltpu.make_async_copy(state_ref.at[row], wide.at[pl.ds(base, CB)], sems.at[row + 1])
+        )
+    copies.append(pltpu.make_async_copy(source_hbm, source_ref, sems.at[SB + 1]))
+    for copy in copies:
+        copy.start()
+    for n in range(2 * (SB - 2)):
+        fetch_end(n).start()
+    for slot in range(2):
+        fetch(slot * (SB - 1), slot).start()
     wide[0:CB, :] = below_ref[...]
     wide[(SB + 1) * 16 : (SB + 1) * 16 + CB, :] = above_ref[...]
     for row, base in enumerate([16, 32, 48, 64, 0, (SB + 1) * 16]):
         wide[base + 8 : base + 9, :] = left_ref[row : row + 1, :]
         wide[base + 9 : base + 10, :] = right_ref[row : row + 1, :]
+    partial[...] = jnp.zeros(partial.shape, jnp.float32)
     for copy in copies:
         copy.wait()
-    late.wait()
-
-    def block_row(p, carry):
-        fetch(p).wait()
+    for p in range(1, SB - 1):
+        for end in range(2):
+            n, q = 2 * (p - 1) + end, end * (CB - 1)
+            fetch_end(n).wait()
+            weigh(ends_ref.at[n], choose(cols_ref, p, q, wide, chosen), partial, q)
+        for v in range(NV):
+            lanes = slice(v * BLK, (v + 1) * BLK)
+            out_ref[p, :, lanes] = source_ref[p, :, lanes] - (inner_ref[p - 1, :, lanes] + sum_slots(partial, v))
+
+    def block_row(slot, carry):
+        p = slot * (SB - 1)
+        fetch(p, slot).wait()
         for q in range(CB):
-            for k in range(K):
-                code = cols_ref[p, k, q]
-                a = lax.shift_right_logical(code * 11, 5)
-                side = q + code - 3 * a - 1
-                column = jnp.where(side < 0, CB, jnp.where(side == CB, CB + 1, side))
-                row = (p + a) * 16 + column
-                chosen[q * 8 + k : q * 8 + k + 1, :] = wide[pl.ds(row, 1), :]
-            inputs = chosen[q * 8 : q * 8 + K, :]
-            for v in range(NV):
-                total = sum_pairs(tiles_ref[p, q, v].astype(jnp.float32) * inputs)
-                for n in range(2 * BLK // LANES):
-                    at = v * CB * K + q * K
-                    partial[n, at : at + K, :] = total[:, n * LANES : (n + 1) * LANES]
+            weigh(rows_ref.at[slot, q], choose(cols_ref, p, q, wide, chosen), partial, q)
         for v in range(NV):
             lanes = slice(v * BLK, (v + 1) * BLK)
-            total = None
-            for k in range(K):
-                rows = pl.ds(v * CB * K + k, CB, stride=K)
-                one = jnp.concatenate([partial[n, rows, :] for n in range(2 * BLK // LANES)], axis=1)
-                total = one if total is None else total + one
-            out_ref[p, :, lanes] = source_ref[p, :, lanes] - fold_pair(total)
+            out_ref[p, :, lanes] = source_ref[p, :, lanes] - sum_slots(partial, v)
         return carry
 
-    lax.fori_loop(0, SB, block_row, 0)
+    lax.fori_loop(0, 2, block_row, 0)
 
 
 def finish(base_ref, spectral_ref, state_ref, inverse_ref, coef_ref, dst_ref, residual_ref, next_ref, lagged):
@@ -310,24 +368,46 @@
     )(who, received)
 
 
-def tile_call(cols, tiles, state, left, right, below, above, source):
-    in_vmem, raw = pl.BlockSpec(memory_space=pltpu.VMEM), pl.BlockSpec(memory_space=pl.ANY)
-    return pl.pallas_call(
-        tile_kernel,
-        out_shape=STATE,
-        in_specs=[raw] * 3 + [in_vmem] * 4 + [raw],
+TILE_SCRATCH = [
+    pltpu.VMEM(((SB + 2) * 16, WIDTH), jnp.float32),
+    pltpu.VMEM((CB * 8, WIDTH), jnp.float32),
+    pltpu.VMEM((2 * BLK // LANES, NV * CB * K, LANES), jnp.float32),
+    pltpu.SemaphoreType.DMA((SB + 2,)),
+]
+
+
+def inner_call(cols, tiles, state):
+    return pl.pallas_call(
+        inner_kernel,
+        out_shape=f32(SB - 2, CB, WIDTH),
+        in_specs=[pl.BlockSpec(memory_space=pl.ANY)] * 3,
         scratch_shapes=[
             pltpu.SMEM(cols.shape, cols.dtype),
-            pltpu.VMEM(tiles.shape, tiles.dtype),
-            pltpu.VMEM(source.shape, source.dtype),
-            pltpu.VMEM(((SB + 2) * 16, WIDTH), jnp.float32),
-            pltpu.VMEM((CB * 8, WIDTH), jnp.float32),
-            pltpu.VMEM((2 * BLK // LANES, NV * CB * K, LANES), jnp.float32),
-            pltpu.SemaphoreType.DMA((SB + 2,)),
+            pltpu.VMEM((SB, CB - 2, *tiles.shape[2:]), tiles.dtype),
+            *TILE_SCRATCH,
             pltpu.SemaphoreType.DMA((SB,)),
         ],
         compiler_params=room(8),
-    )(in_hbm(cols), in_hbm(tiles), state, left, right, below, above, in_hbm(source))
+    )(in_hbm(cols), in_hbm(tiles), state)
+
+
+def outer_call(cols, tiles, state, left, right, below, above, source, inner):
+    in_vmem, raw = pl.BlockSpec(memory_space=pltpu.VMEM), pl.BlockSpec(memory_space=pl.ANY)
+    return pl.pallas_call(
+        outer_kernel,
+        out_shape=STATE,
+        in_specs=[raw] * 3 + [in_vmem] * 4 + [raw, in_vmem],
+        scratch_shapes=[
+            pltpu.SMEM(cols.shape, cols.dtype),
+            pltpu.VMEM((2, *tiles.shape[1:]), tiles.dtype),
+            pltpu.VMEM((2 * (SB - 2), *tiles.shape[2:]), tiles.dtype),
+            pltpu.VMEM(source.shape, source.dtype),
+            *TILE_SCRATCH,
+            pltpu.SemaphoreType.DMA((2,)),
+            pltpu.SemaphoreType.DMA((2 * (SB - 2),)),
+        ],
+        compiler_params=room(8),
+    )(in_hbm(cols), in_hbm(tiles), state, left, right, below, above, in_hbm(source), inner)
 
 
 def finish_specs(count):
@@ -355,7 +435,7 @@
 
 
 def exchange(array):
-    return lax.all_to_all(array, "inst", 0, 0, tiled=True)
+    return lax.all_to_all(array, "inst", 0, 0, tiled=True, axis_index_groups=[list(OWNER)])
 
 
 def halos(state, low_edge, high_edge):
@@ -381,8 +461,11 @@
     for sweep in range(SWEEPS):
         received = exchange(send.reshape(NT, SHARE, LANES))
         left, right, below, above = halos(state, low_edge, high_edge)
+        placed = in_hbm(state) if sweep == 0 else state
+        inner = inner_call(tile_cols, tiles, placed)
+        received, inner = lax.optimization_barrier((received, inner))
         spectral = exchange(spectral_call(who, received)).reshape(NT * SHARE, LANES)
-        base = tile_call(tile_cols, tiles, in_hbm(state) if sweep == 0 else state, left, right, below, above, source)
+        base = outer_call(tile_cols, tiles, placed, left, right, below, above, source, inner)
         if sweep < SWEEPS - 1:
             state, send, low_edge, high_edge = middle_call(
                 base, spectral, state, inverse, coef, face_dst, face_src

time: 115 us -> 113 us (0.983)
  the two profiles are of different devices: /device:TPU:52 before, /device:TPU:34 now
where the time goes in v3:
time: 113 us; the launch traced here: 112 us
  starting transfers between devices  61.5 us (54%)
  waiting for transfers between devices  30.6 us (27%)
  Pallas kernels  18.1 us (16%)
    all_to_all x4, starting transfers between devices, exchange(): lax.all_to_all(array, 'inst', 0, 0, tiled=True, axis_index_groups=[list(O...  35.7 us
    all_to_all x4, waiting for transfers between devices, exchange(): lax.all_to_all(array, 'inst', 0, 0, tiled=True, axis_index_groups=[list(O...  23.6 us
    ppermute x2, starting transfers between devices, halos(): lax.ppermute(high_edge, 'chord', [(i, (i - 1) % n) for i in range(n)])  8.53 us
    ppermute x2, starting transfers between devices, halos(): above = lax.ppermute(state[0], 'span', [(i + 1, i) for i in range(n - 1)])  7.41 us
    pallas_call x2, Pallas kernels, outer_call(): pl.pallas_call(outer_kernel, out_shape=STATE, in_specs=[raw] * 3 + [in_vm...  6.08 us
    ppermute x2, starting transfers between devices, halos(): lax.ppermute(state[SB - 1], 'span', [(i, i + 1) for i in range(n - 1)])  6.07 us
    ppermute x2, waiting for transfers between devices, halos(): left = lax.ppermute(low_edge, 'chord', [(i, (i + 1) % n) for i in range(n)])  5.11 us
    pallas_call x2, Pallas kernels, inner_call(): pl.pallas_call(inner_kernel, out_shape=f32(SB - 2, CB, WIDTH), in_specs=[...  4.26 us
  transfers between devices with their start and end apart: 12, of which 6 were waited for; matrix products, arithmetic and copies ran while one was open for 1% of the time, Pallas kernels for 11%

profile of v3, /device:TPU:34, one launch (start us, length us, event | category | flops | bytes accessed | tf_op | source)
XLA Modules:
  0.0 112.1 jit_solution(8181307800505002167)
XLA Ops:
  0.6 2.2 %shard_map.95 = (f32[512,128]{1,0:T(8,128)}, f32[4,1920]{1,0:T(4,128)S(1)}, f32[4,1920]{1,0:T(4,128)S(1)}) custom-call(f32[4,8,1920]{2,1,0:T(8,128)} %bitcast.25, s32[2,256]{1,0:T(2,128)} %src_ref.3), custom_call_target="tpu_custom_call" | custom-call | tf_op jit(solution)/shard_map/pallas_call | solution.py:349
  2.8 15.2 %all-to-all-start = ((f32[16,32,128]{2,1,0:T(8,128)}), f32[16,32,128]{2,1,0:T(8,128)S(1)}, u32[]{:S(2)}, u32[]{:S(2)}) async-start(f32[16,32,128]{2,1,0:T(8,128)} %bitcast.8), calls=%async_computation | async-start | bytes 524288 | tf_op jit(solution)/shard_map/all_to_all | solution.py:438
  18.1 0.9 slice_bitcast_fusion.3
  18.9 3.5 %collective-permute-start = (f32[8,1920]{1,0:T(8,128)S(1)}, f32[8,1920]{1,0:T(8,128)S(1)}, u32[]{:S(2)}, u32[]{:S(2)}) collective-permute-start(f32[8,1920]{1,0:T(8,128)S(1)} %get-tuple-element.30), channel_id=1, source_target_pairs={{0,4},{4,8},{8,12},{12,16},{16,20},{20,24},{24,28},{1,5},{5,9},{9,... | collective-permute-start | bytes 184328 | tf_op jit(solution)/shard_map/ppermute | solution.py:443
  22.4 3.3 %collective-permute-start.1 = (f32[8,1920]{1,0:T(8,128)S(1)}, f32[8,1920]{1,0:T(8,128)S(1)}, u32[]{:S(2)}, u32[]{:S(2)}) collective-permute-start(f32[8,1920]{1,0:T(8,128)S(1)} %get-tuple-element.31), channel_id=1, source_target_pairs={{4,0},{8,4},{12,8},{16,12},{20,16},{24,20},{28,24},{5,1},{9,5},{13... | collective-permute-start | bytes 184328 | tf_op jit(solution)/shard_map/ppermute | solution.py:444
  25.7 2.0 %shard_map.96.inner_ref = f32[2,8,1920]{2,1,0:T(8,128)S(1)} custom-call(s32[4,4,8]{2,1,0:T(4,128)} %bitcast.41, bf16[4,8,6,4,1920]{4,3,2,1,0:T(4,128)(2,1)} %bitcast.35, f32[4,8,1920]{2,1,0:T(8,128)} %bitcast.26), custom_call_target="tpu_custom_call" | custom-call | tf_op jit(solution)/shard_map/pallas_call | solution.py:380
  27.7 0.0 copy-start
  27.8 0.0 copy-start.1
  27.8 0.0 copy-start.2
  27.8 0.0 copy-start.3
  27.8 0.0 copy-start.4
  27.8 8.0 %all-to-all-done.in_ref = f32[16,32,128]{2,1,0:T(8,128)S(1)} async-done(((f32[16,32,128]{2,1,0:T(8,128)}), f32[16,32,128]{2,1,0:T(8,128)S(1)}, u32[]{:S(2)}, u32[]{:S(2)}) %all-to-all-start) | async-done | bytes 262176 | tf_op jit(solution)/shard_map/all_to_all | solution.py:438
  35.8 0.9 shard_map.98
  36.7 6.4 %all-to-all-start.1 = ((f32[16,32,128]{2,1,0:T(8,128)}), f32[16,32,128]{2,1,0:T(8,128)S(1)}, u32[]{:S(2)}, u32[]{:S(2)}) async-start(f32[16,32,128]{2,1,0:T(8,128)} %shard_map.98), calls=%async_computation.1 | async-start | bytes 524288 | tf_op jit(solution)/shard_map/all_to_all | solution.py:438
  43.1 0.0 collective-permute-done.below_ref
  43.1 0.0 collective-permute-done.1.above_ref
  43.2 3.4 %collective-permute-start.3 = (f32[6,1920]{1,0:T(8,128)S(1)}, f32[6,1920]{1,0:T(8,128)S(1)}, u32[]{:S(2)}, u32[]{:S(2)}) collective-permute-start(f32[6,1920]{1,0:T(8,128)S(1)} %pad_maximum_fusion.1), channel_id=1, source_target_pairs={{0,3},{1,0},{2,1},{3,2},{4,7},{5,4},{6,5},{7,6},{8,11},{9,8},{10,9... | collective-permute-start | bytes 138248 | tf_op jit(solution)/shard_map/ppermute | solution.py:449
  46.6 1.9 %collective-permute-start.2 = (f32[6,1920]{1,0:T(8,128)S(1)}, f32[6,1920]{1,0:T(8,128)S(1)}, u32[]{:S(2)}, u32[]{:S(2)}) collective-permute-start(f32[6,1920]{1,0:T(8,128)S(1)} %pad_maximum_fusion), channel_id=1, source_target_pairs={{0,1},{1,2},{2,3},{3,0},{4,5},{5,6},{6,7},{7,4},{8,9},{9,10},{10,1... | collective-permute-start | bytes 138248 | tf_op jit(solution)/shard_map/ppermute | solution.py:448
  48.5 0.0 collective-permute-done.3.right_ref
  48.5 5.1 %collective-permute-done.2.left_ref = f32[6,1920]{1,0:T(8,128)S(1)} collective-permute-done((f32[6,1920]{1,0:T(8,128)S(1)}, f32[6,1920]{1,0:T(8,128)S(1)}, u32[]{:S(2)}, u32[]{:S(2)}) %collective-permute-start.2) | collective-permute-done | bytes 46112 | tf_op jit(solution)/shard_map/ppermute | solution.py:448
  53.6 3.0 %shard_map.97.base_ref = f32[4,8,1920]{2,1,0:T(8,128)S(1)} custom-call(s32[4,4,8]{2,1,0:T(4,128)} %bitcast.42, bf16[4,8,6,4,1920]{4,3,2,1,0:T(4,128)(2,1)} %bitcast.36, f32[4,8,1920]{2,1,0:T(8,128)} %bitcast.27, f32[6,1920]{1,0:T(8,128)S(1)} %collective-permute-done.2.left_ref, f32[6,1920]{1,0:T(8,128)S(1)} %collective-permute-done.3.right_ref, ...), custom_call_target="tpu_custom_call" | custom-call | tf_op jit(solution)/shard_map/pallas_call | solution.py:396
  56.6 3.7 %all-to-all-done.1 = f32[16,32,128]{2,1,0:T(8,128)S(1)} async-done(((f32[16,32,128]{2,1,0:T(8,128)}), f32[16,32,128]{2,1,0:T(8,128)S(1)}, u32[]{:S(2)}, u32[]{:S(2)}) %all-to-all-start.1) | async-done | bytes 262176 | tf_op jit(solution)/shard_map/all_to_all | solution.py:438
  60.3 0.0 copy-done
  60.3 0.0 copy-done.1
  60.3 0.0 copy-done.2
  60.3 0.0 copy-done.3
  60.3 0.0 copy-done.4
  60.4 2.2 %shard_map.99 = (f32[4,8,1920]{2,1,0:T(8,128)S(1)}, f32[512,128]{1,0:T(8,128)}, f32[4,1920]{1,0:T(4,128)S(1)}, f32[4,1920]{1,0:T(4,128)S(1)}) custom-call(f32[4,8,1920]{2,1,0:T(8,128)S(1)} %shard_map.97.base_ref, f32[512,128]{1,0:T(8,128)S(1)} %bitcast.31, f32[4,8,1920]{2,1,0:T(8,128)S(1)} %bitcast.28, bf16[4,6,8,1920]{3,2,1,0:T(8,128)(2,1)S(1)} %bitcast.29, ...), custom_call_target="tpu_custom_call" | custom-call | tf_op jit(solution)/shard_map/pallas_call | solution.py:418
  62.5 8.3 %all-to-all-start.2 = ((f32[16,32,128]{2,1,0:T(8,128)}), f32[16,32,128]{2,1,0:T(8,128)S(1)}, u32[]{:S(2)}, u32[]{:S(2)}) async-start(f32[16,32,128]{2,1,0:T(8,128)} %bitcast.16), calls=%async_computation.2 | async-start | bytes 524288 | tf_op jit(solution)/shard_map/all_to_all | solution.py:438
  70.9 2.6 %collective-permute-start.4 = (f32[8,1920]{1,0:T(8,128)S(1)}, f32[8,1920]{1,0:T(8,128)S(1)}, u32[]{:S(2)}, u32[]{:S(2)}) collective-permute-start(f32[8,1920]{1,0:T(8,128)S(1)} %get-tuple-element.28), channel_id=1, source_target_pairs={{0,4},{4,8},{8,12},{12,16},{16,20},{20,24},{24,28},{1,5},{5,9},{9,... | collective-permute-start | bytes 184328 | tf_op jit(solution)/shard_map/ppermute | solution.py:443
  73.5 2.2 %shard_map.100.inner_ref = f32[2,8,1920]{2,1,0:T(8,128)S(1)} custom-call(s32[4,4,8]{2,1,0:T(4,128)} %bitcast.43, bf16[4,8,6,4,1920]{4,3,2,1,0:T(4,128)(2,1)} %bitcast.37, f32[4,8,1920]{2,1,0:T(8,128)S(1)} %get-tuple-element.20.state_ref), custom_call_target="tpu_custom_call" | custom-call | tf_op jit(solution)/shard_map/pallas_call | solution.py:380
  75.7 4.2 %collective-permute-start.5 = (f32[8,1920]{1,0:T(8,128)S(1)}, f32[8,1920]{1,0:T(8,128)S(1)}, u32[]{:S(2)}, u32[]{:S(2)}) collective-permute-start(f32[8,1920]{1,0:T(8,128)S(1)} %get-tuple-element.29), channel_id=1, source_target_pairs={{4,0},{8,4},{12,8},{16,12},{20,16},{24,20},{28,24},{5,1},{9,5},{13... | collective-permute-start | bytes 184328 | tf_op jit(solution)/shard_map/ppermute | solution.py:444
  79.9 7.6 %all-to-all-done.2.in_ref = f32[16,32,128]{2,1,0:T(8,128)S(1)} async-done(((f32[16,32,128]{2,1,0:T(8,128)}), f32[16,32,128]{2,1,0:T(8,128)S(1)}, u32[]{:S(2)}, u32[]{:S(2)}) %all-to-all-start.2) | async-done | bytes 262176 | tf_op jit(solution)/shard_map/all_to_all | solution.py:438
  87.5 0.9 shard_map.102
  88.4 5.7 %all-to-all-start.3 = ((f32[16,32,128]{2,1,0:T(8,128)}), f32[16,32,128]{2,1,0:T(8,128)S(1)}, u32[]{:S(2)}, u32[]{:S(2)}) async-start(f32[16,32,128]{2,1,0:T(8,128)} %shard_map.102), calls=%async_computation.3 | async-start | bytes 524288 | tf_op jit(solution)/shard_map/all_to_all | solution.py:438
  94.1 0.0 collective-permute-done.4.below_ref
  94.1 0.0 collective-permute-done.5.above_ref
  94.2 1.9 %collective-permute-start.6 = (f32[6,1920]{1,0:T(8,128)S(1)}, f32[6,1920]{1,0:T(8,128)S(1)}, u32[]{:S(2)}, u32[]{:S(2)}) collective-permute-start(f32[6,1920]{1,0:T(8,128)S(1)} %pad_maximum_fusion.2), channel_id=1, source_target_pairs={{0,1},{1,2},{2,3},{3,0},{4,5},{5,6},{6,7},{7,4},{8,9},{9,10},{10,1... | collective-permute-start | bytes 138248 | tf_op jit(solution)/shard_map/ppermute | solution.py:448
  96.1 5.1 %collective-permute-start.7 = (f32[6,1920]{1,0:T(8,128)S(1)}, f32[6,1920]{1,0:T(8,128)S(1)}, u32[]{:S(2)}, u32[]{:S(2)}) collective-permute-start(f32[6,1920]{1,0:T(8,128)S(1)} %pad_maximum_fusion.3), channel_id=1, source_target_pairs={{0,3},{1,0},{2,1},{3,2},{4,7},{5,4},{6,5},{7,6},{8,11},{9,8},{10,9... | collective-permute-start | bytes 138248 | tf_op jit(solution)/shard_map/ppermute | solution.py:449
  101.3 0.0 collective-permute-done.6.left_ref
  101.3 1.8 %collective-permute-done.7.right_ref = f32[6,1920]{1,0:T(8,128)S(1)} collective-permute-done((f32[6,1920]{1,0:T(8,128)S(1)}, f32[6,1920]{1,0:T(8,128)S(1)}, u32[]{:S(2)}, u32[]{:S(2)}) %collective-permute-start.7) | collective-permute-done | bytes 46112 | tf_op jit(solution)/shard_map/ppermute | solution.py:449
  103.1 3.1 %shard_map.101.base_ref = f32[4,8,1920]{2,1,0:T(8,128)S(1)} custom-call(s32[4,4,8]{2,1,0:T(4,128)} %bitcast.44, bf16[4,8,6,4,1920]{4,3,2,1,0:T(4,128)(2,1)} %bitcast.38, f32[4,8,1920]{2,1,0:T(8,128)S(1)} %get-tuple-element.20.state_ref, f32[6,1920]{1,0:T(8,128)S(1)} %collective-permute-done.6.left_ref, f32[6,1920]{1,0:T(8,128)S(1)} %collective-permute-done.7.right_ref, ...), custom_call_target="tpu_custom_call" | custom-call | tf_op jit(solution)/shard_map/pallas_call | solution.py:396
  106.2 4.3 %all-to-all-done.3 = f32[16,32,128]{2,1,0:T(8,128)S(1)} async-done(((f32[16,32,128]{2,1,0:T(8,128)}), f32[16,32,128]{2,1,0:T(8,128)S(1)}, u32[]{:S(2)}, u32[]{:S(2)}) %all-to-all-start.3) | async-done | bytes 262176 | tf_op jit(solution)/shard_map/all_to_all | solution.py:438
  110.5 1.6 %shard_map.103 = (f32[4,8,1920]{2,1,0:T(8,128)}, f32[4,8,1920]{2,1,0:T(8,128)}) custom-call(f32[4,8,1920]{2,1,0:T(8,128)S(1)} %shard_map.101.base_ref, f32[512,128]{1,0:T(8,128)S(1)} %bitcast.32, f32[4,8,1920]{2,1,0:T(8,128)S(1)} %get-tuple-element.20.state_ref, bf16[4,6,8,1920]{3,2,1,0:T(8,128)(2,1)S(1)} %bitcast.30, bf16[72,256]{1,0:T(8,128)(2,1)S(1)} %bitcast.34, ...), custom_call_target="tpu_custom_call" | custom-call | tf_op jit(solution)/shard_map/pallas_call | solution.py:428
  (9 shorter events, 0.2 us)
Async XLA Ops:
  2.8 33.0 %all-to-all-start = ((f32[16,32,128]{2,1,0:T(8,128)}), f32[16,32,128]{2,1,0:T(8,128)S(1)}, u32[]{:S(2)}, u32[]{:S(2)}) async-start(f32[16,32,128]{2,1,0:T(8,128)} %bitcast.8), calls=%async_computation | async-start | bytes 524288 | tf_op jit(solution)/shard_map/all_to_all | solution.py:438
  18.9 24.1 %collective-permute-start = (f32[8,1920]{1,0:T(8,128)S(1)}, f32[8,1920]{1,0:T(8,128)S(1)}, u32[]{:S(2)}, u32[]{:S(2)}) collective-permute-start(f32[8,1920]{1,0:T(8,128)S(1)} %get-tuple-element.30), channel_id=1, source_target_pairs={{0,4},{4,8},{8,12},{12,16},{16,20},{20,24},{24,28},{1,5},{5,9},{9,... | collective-permute-start | bytes 184328 | tf_op jit(solution)/shard_map/ppermute | solution.py:443
  22.4 20.7 %collective-permute-start.1 = (f32[8,1920]{1,0:T(8,128)S(1)}, f32[8,1920]{1,0:T(8,128)S(1)}, u32[]{:S(2)}, u32[]{:S(2)}) collective-permute-start(f32[8,1920]{1,0:T(8,128)S(1)} %get-tuple-element.31), channel_id=1, source_target_pairs={{4,0},{8,4},{12,8},{16,12},{20,16},{24,20},{28,24},{5,1},{9,5},{13... | collective-permute-start | bytes 184328 | tf_op jit(solution)/shard_map/ppermute | solution.py:444
  27.7 32.6 %copy-start = (f32[1,4,8,1920]{3,2,1,0:T(8,128)S(1)}, f32[1,4,8,1920]{3,2,1,0:T(8,128)}, u32[]{:S(2)}) copy-start(f32[1,4,8,1920]{3,2,1,0:T(8,128)} %param.9) | copy-start | bytes 737284
  27.8 32.6 %copy-start.1 = (bf16[1,4,8,6,1920]{4,2,3,1,0:T(8,128)(2,1)S(1)}, bf16[1,4,8,6,1920]{4,2,3,1,0:T(8,128)(2,1)}, u32[]{:S(2)}) copy-start(bf16[1,4,8,6,1920]{4,2,3,1,0:T(8,128)(2,1)} %param.12) | copy-start | bytes 2211844
  27.8 32.6 %copy-start.2 = (bf16[1,72,256]{2,1,0:T(8,128)(2,1)S(1)}, bf16[1,72,256]{2,1,0:T(8,128)(2,1)}, u32[]{:S(2)}) copy-start(bf16[1,72,256]{2,1,0:T(8,128)(2,1)} %param.15) | copy-start | bytes 110596
  27.8 32.6 %copy-start.3 = (s32[2,256]{1,0:T(2,128)S(1)}, s32[2,256]{1,0:T(2,128)}, u32[]{:S(2)}) copy-start(s32[2,256]{1,0:T(2,128)} %src_ref.3) | copy-start | bytes 6148
  27.8 32.6 %copy-start.4 = (s32[2,256]{1,0:T(2,128)S(1)}, s32[2,256]{1,0:T(2,128)}, u32[]{:S(2)}) copy-start(s32[2,256]{1,0:T(2,128)} %dst_ref.3) | copy-start | bytes 6148
  36.7 23.6 %all-to-all-start.1 = ((f32[16,32,128]{2,1,0:T(8,128)}), f32[16,32,128]{2,1,0:T(8,128)S(1)}, u32[]{:S(2)}, u32[]{:S(2)}) async-start(f32[16,32,128]{2,1,0:T(8,128)} %shard_map.98), calls=%async_computation.1 | async-start | bytes 524288 | tf_op jit(solution)/shard_map/all_to_all | solution.py:438
  43.2 5.4 %collective-permute-start.3 = (f32[6,1920]{1,0:T(8,128)S(1)}, f32[6,1920]{1,0:T(8,128)S(1)}, u32[]{:S(2)}, u32[]{:S(2)}) collective-permute-start(f32[6,1920]{1,0:T(8,128)S(1)} %pad_maximum_fusion.1), channel_id=1, source_target_pairs={{0,3},{1,0},{2,1},{3,2},{4,7},{5,4},{6,5},{7,6},{8,11},{9,8},{10,9... | collective-permute-start | bytes 138248 | tf_op jit(solution)/shard_map/ppermute | solution.py:449
  46.6 7.0 %collective-permute-start.2 = (f32[6,1920]{1,0:T(8,128)S(1)}, f32[6,1920]{1,0:T(8,128)S(1)}, u32[]{:S(2)}, u32[]{:S(2)}) collective-permute-start(f32[6,1920]{1,0:T(8,128)S(1)} %pad_maximum_fusion), channel_id=1, source_target_pairs={{0,1},{1,2},{2,3},{3,0},{4,5},{5,6},{6,7},{7,4},{8,9},{9,10},{10,1... | collective-permute-start | bytes 138248 | tf_op jit(solution)/shard_map/ppermute | solution.py:448
  62.5 25.0 %all-to-all-start.2 = ((f32[16,32,128]{2,1,0:T(8,128)}), f32[16,32,128]{2,1,0:T(8,128)S(1)}, u32[]{:S(2)}, u32[]{:S(2)}) async-start(f32[16,32,128]{2,1,0:T(8,128)} %bitcast.16), calls=%async_computation.2 | async-start | bytes 524288 | tf_op jit(solution)/shard_map/all_to_all | solution.py:438
  70.9 23.2 %collective-permute-start.4 = (f32[8,1920]{1,0:T(8,128)S(1)}, f32[8,1920]{1,0:T(8,128)S(1)}, u32[]{:S(2)}, u32[]{:S(2)}) collective-permute-start(f32[8,1920]{1,0:T(8,128)S(1)} %get-tuple-element.28), channel_id=1, source_target_pairs={{0,4},{4,8},{8,12},{12,16},{16,20},{20,24},{24,28},{1,5},{5,9},{9,... | collective-permute-start | bytes 184328 | tf_op jit(solution)/shard_map/ppermute | solution.py:443
  75.7 18.4 %collective-permute-start.5 = (f32[8,1920]{1,0:T(8,128)S(1)}, f32[8,1920]{1,0:T(8,128)S(1)}, u32[]{:S(2)}, u32[]{:S(2)}) collective-permute-start(f32[8,1920]{1,0:T(8,128)S(1)} %get-tuple-element.29), channel_id=1, source_target_pairs={{4,0},{8,4},{12,8},{16,12},{20,16},{24,20},{28,24},{5,1},{9,5},{13... | collective-permute-start | bytes 184328 | tf_op jit(solution)/shard_map/ppermute | solution.py:444
  88.4 22.2 %all-to-all-start.3 = ((f32[16,32,128]{2,1,0:T(8,128)}), f32[16,32,128]{2,1,0:T(8,128)S(1)}, u32[]{:S(2)}, u32[]{:S(2)}) async-start(f32[16,32,128]{2,1,0:T(8,128)} %shard_map.102), calls=%async_computation.3 | async-start | bytes 524288 | tf_op jit(solution)/shard_map/all_to_all | solution.py:438
  94.2 7.1 %collective-permute-start.6 = (f32[6,1920]{1,0:T(8,128)S(1)}, f32[6,1920]{1,0:T(8,128)S(1)}, u32[]{:S(2)}, u32[]{:S(2)}) collective-permute-start(f32[6,1920]{1,0:T(8,128)S(1)} %pad_maximum_fusion.2), channel_id=1, source_target_pairs={{0,1},{1,2},{2,3},{3,0},{4,5},{5,6},{6,7},{7,4},{8,9},{9,10},{10,1... | collective-permute-start | bytes 138248 | tf_op jit(solution)/shard_map/ppermute | solution.py:448
  96.1 7.0 %collective-permute-start.7 = (f32[6,1920]{1,0:T(8,128)S(1)}, f32[6,1920]{1,0:T(8,128)S(1)}, u32[]{:S(2)}, u32[]{:S(2)}) collective-permute-start(f32[6,1920]{1,0:T(8,128)S(1)} %pad_maximum_fusion.3), channel_id=1, source_target_pairs={{0,3},{1,0},{2,1},{3,2},{4,7},{5,4},{6,5},{7,6},{8,11},{9,8},{10,9... | collective-permute-start | bytes 138248 | tf_op jit(solution)/shard_map/ppermute | solution.py:449

commit v4 on v3

--- a/solution.py
+++ b/solution.py
@@ -138,17 +138,6 @@
             out_ref[SLOT[t], 16:32, :] = in_ref[SLOT[(t + LAG) % NT], 16:32, :]
 
 
-def put(ref, row, count, value):
-    ref[0, pl.ds(row, count), :] = value[:, :LANES]
-    ref[1, pl.ds(row, count), :] = value[:, LANES : 2 * LANES]
-    ref[2, pl.ds(row, count), 0 : BLK - 2 * LANES] = value[:, 2 * LANES :]
-
-
-def take(ref, row):
-    parts = [ref[n, pl.ds(row, CB, stride=8), :] for n in range(3)]
-    return jnp.concatenate(parts, axis=1)[:, :BLK]
-
-
 def fold_pair(total):
     return total[:, :BLK] + total[:, BLK:]
 
@@ -270,61 +259,59 @@
     lax.fori_loop(0, 2, block_row, 0)
 
 
-def finish(base_ref, spectral_ref, state_ref, inverse_ref, coef_ref, dst_ref, residual_ref, next_ref, lagged):
+def finish(base_ref, spectral_ref, state_ref, inverse_ref, coef_ref, dst_ref, residual_ref, next_ref):
     coef = coef_ref[...].astype(jnp.float32)
     spread, cells = [], []
+    blocks = SB * CB
     for side in range(2):
         row = FACE_ROW + side * 16
         pack = jnp.concatenate([spectral_ref[row : row + NV, :], spectral_ref[row + 8 : row + 8 + NV, :]], axis=1)
-        contrib = []
+        block, cell = split_cells(dst_ref[side : side + 1, :])
+        mine = lax.broadcasted_iota(jnp.int32, (blocks, PF), 0) == block
+        placed = []
         for v in range(NV):
             at = (side * NV + v) * NV
-            contrib.append(jnp.sum(coef[at : at + NV] * pack, axis=0, keepdims=True))
-        contrib = jnp.concatenate(contrib + [jnp.zeros((8 - NV, PF), jnp.float32)], axis=0)
-        block, cell = split_cells(dst_ref[side : side + 1, :])
-        spread.append(
-            jnp.concatenate([jnp.where(block == b, contrib, 0.0) for b in range(SB * CB)], axis=0)
-        )
+            contrib = jnp.sum(coef[at : at + NV] * pack, axis=0, keepdims=True)
+            placed.append(jnp.where(mine, contrib, 0.0))
+        spread.append(jnp.concatenate(placed, axis=0))
         cells.append(one_hot(BLK, cell))
     stacked = jnp.concatenate(three_parts(jnp.concatenate(spread, axis=1)), axis=0)
-    placed = lax.dot_general(
+    lag = lax.dot_general(
         stacked,
         jnp.concatenate(cells, axis=1),
         (((1,), (1,)), ((), ())),
         preferred_element_type=jnp.float32,
     )
-    count = SB * CB * 8
-    put(lagged, 0, count, placed[:count] + (placed[count : 2 * count] + placed[2 * count :]))
+    count = NV * blocks
+    lag = lag[:count] + (lag[count : 2 * count] + lag[2 * count :])
     for p in range(SB):
         first = p * STRIPS * 8
         spectral = jnp.concatenate(
             [spectral_ref[first + 8 * n : first + 8 * n + 8, :] for n in range(STRIPS)], axis=1
         )
-        residual_ref[p] = base_ref[p] - spectral
-        for v in range(NV):
-            lanes = slice(v * BLK, (v + 1) * BLK)
-            residual_ref[p, :, lanes] = (
-                residual_ref[p, :, lanes] - take(lagged, p * CB * 8 + v)
-            )
-
-        for v in range(NV):
-            lanes = slice(v * BLK, (v + 1) * BLK)
-            product = inverse_ref[p, v].astype(jnp.float32) * residual_ref[p]
-            next_ref[p, :, lanes] = state_ref[p, :, lanes] + fold_pair(sum_pairs(product))
+        lagged = jnp.concatenate(
+            [lag[v * blocks + p * CB : v * blocks + (p + 1) * CB] for v in range(NV)], axis=1
+        )
+        residual = base_ref[p] - spectral - lagged
+        residual_ref[p] = residual
+        change = [
+            fold_pair(sum_pairs(inverse_ref[p, v].astype(jnp.float32) * residual)) for v in range(NV)
+        ]
+        next_ref[p] = state_ref[p] + jnp.concatenate(change, axis=1)
 
 
 def middle_kernel(
-    base_ref, spectral_ref, state_ref, inverse_ref, coef_ref, dst_ref, src_ref, next_ref, send_ref, low_ref, high_ref, residual_ref, lagged
+    base_ref, spectral_ref, state_ref, inverse_ref, coef_ref, dst_ref, src_ref, next_ref, send_ref, low_ref, high_ref, residual_ref
 ):
-    finish(base_ref, spectral_ref, state_ref, inverse_ref, coef_ref, dst_ref, residual_ref, next_ref, lagged)
+    finish(base_ref, spectral_ref, state_ref, inverse_ref, coef_ref, dst_ref, residual_ref, next_ref)
     emit_exchange(next_ref, src_ref, send_ref)
     emit_edges(next_ref, low_ref, high_ref)
 
 
 def last_kernel(
-    base_ref, spectral_ref, state_ref, inverse_ref, coef_ref, dst_ref, next_ref, residual_ref, lagged
+    base_ref, spectral_ref, state_ref, inverse_ref, coef_ref, dst_ref, next_ref, residual_ref
 ):
-    finish(base_ref, spectral_ref, state_ref, inverse_ref, coef_ref, dst_ref, residual_ref, next_ref, lagged)
+    finish(base_ref, spectral_ref, state_ref, inverse_ref, coef_ref, dst_ref, residual_ref, next_ref)
 
 
 def f32(*shape):
@@ -334,9 +321,6 @@
 STATE = f32(SB, CB, WIDTH)
 EDGE = f32(SB, WIDTH)
 SEND = f32(NT * SHARE, LANES)
-FINISH_SCRATCH = [
-    pltpu.VMEM((3, SB * CB * 8, LANES), jnp.float32),
-]
 def room(mebibytes):
     return pltpu.CompilerParams(vmem_limit_bytes=mebibytes << 20)
 
@@ -419,7 +403,7 @@
         middle_kernel,
         out_shape=(STATE, SEND, EDGE, EDGE),
         in_specs=finish_specs(7),
-        scratch_shapes=[pltpu.VMEM((SB, CB, WIDTH), jnp.float32)] + FINISH_SCRATCH,
+        scratch_shapes=[pltpu.VMEM((SB, CB, WIDTH), jnp.float32)],
         compiler_params=room(8),
     )(base, spectral, state, inverse, coef, dst, src)
 
@@ -429,7 +413,6 @@
         last_kernel,
         out_shape=(STATE, STATE),
         in_specs=finish_specs(6),
-        scratch_shapes=FINISH_SCRATCH,
         compiler_params=room(8),
     )(base, spectral, state, inverse, coef, dst)
 

time: 113 us -> 113 us (level)
  the two profiles are of different devices: /device:TPU:34 before, /device:TPU:38 now
where the time goes in v4:
time: 113 us; the launch traced here: 112 us
  starting transfers between devices  61.5 us (54%)
  waiting for transfers between devices  30.6 us (27%)
  Pallas kernels  17.9 us (16%)
    all_to_all x4, starting transfers between devices, exchange(): lax.all_to_all(array, 'inst', 0, 0, tiled=True, axis_index_groups=[list(O...  35.7 us
    all_to_all x4, waiting for transfers between devices, exchange(): lax.all_to_all(array, 'inst', 0, 0, tiled=True, axis_index_groups=[list(O...  23.6 us
    ppermute x2, starting transfers between devices, halos(): lax.ppermute(high_edge, 'chord', [(i, (i - 1) % n) for i in range(n)])  8.53 us
    ppermute x2, starting transfers between devices, halos(): above = lax.ppermute(state[0], 'span', [(i + 1, i) for i in range(n - 1)])  7.41 us
    pallas_call x2, Pallas kernels, outer_call(): pl.pallas_call(outer_kernel, out_shape=STATE, in_specs=[raw] * 3 + [in_vm...  6.08 us
    ppermute x2, starting transfers between devices, halos(): lax.ppermute(state[SB - 1], 'span', [(i, i + 1) for i in range(n - 1)])  6.07 us
    ppermute x2, waiting for transfers between devices, halos(): left = lax.ppermute(low_edge, 'chord', [(i, (i + 1) % n) for i in range(n)])  5.11 us
    pallas_call x2, Pallas kernels, inner_call(): pl.pallas_call(inner_kernel, out_shape=f32(SB - 2, CB, WIDTH), in_specs=[...  4.26 us
  transfers between devices with their start and end apart: 12, of which 6 were waited for; matrix products, arithmetic and copies ran while one was open for 1% of the time, Pallas kernels for 11%

profile of v4, /device:TPU:38, one launch (start us, length us, event | category | flops | bytes accessed | tf_op | source)
XLA Modules:
  0.0 111.9 jit_solution(761440801830651165)
XLA Ops:
  0.6 2.2 %shard_map.95 = (f32[512,128]{1,0:T(8,128)}, f32[4,1920]{1,0:T(4,128)S(1)}, f32[4,1920]{1,0:T(4,128)S(1)}) custom-call(f32[4,8,1920]{2,1,0:T(8,128)} %bitcast.25, s32[2,256]{1,0:T(2,128)} %src_ref.3), custom_call_target="tpu_custom_call" | custom-call | tf_op jit(solution)/shard_map/pallas_call | solution.py:333
  2.8 15.2 %all-to-all-start = ((f32[16,32,128]{2,1,0:T(8,128)}), f32[16,32,128]{2,1,0:T(8,128)S(1)}, u32[]{:S(2)}, u32[]{:S(2)}) async-start(f32[16,32,128]{2,1,0:T(8,128)} %bitcast.8), calls=%async_computation | async-start | bytes 524288 | tf_op jit(solution)/shard_map/all_to_all | solution.py:421
  18.1 0.9 slice_bitcast_fusion.3
  18.9 3.5 %collective-permute-start = (f32[8,1920]{1,0:T(8,128)S(1)}, f32[8,1920]{1,0:T(8,128)S(1)}, u32[]{:S(2)}, u32[]{:S(2)}) collective-permute-start(f32[8,1920]{1,0:T(8,128)S(1)} %get-tuple-element.30), channel_id=1, source_target_pairs={{0,4},{4,8},{8,12},{12,16},{16,20},{20,24},{24,28},{1,5},{5,9},{9,... | collective-permute-start | bytes 184328 | tf_op jit(solution)/shard_map/ppermute | solution.py:426
  22.4 3.3 %collective-permute-start.1 = (f32[8,1920]{1,0:T(8,128)S(1)}, f32[8,1920]{1,0:T(8,128)S(1)}, u32[]{:S(2)}, u32[]{:S(2)}) collective-permute-start(f32[8,1920]{1,0:T(8,128)S(1)} %get-tuple-element.31), channel_id=1, source_target_pairs={{4,0},{8,4},{12,8},{16,12},{20,16},{24,20},{28,24},{5,1},{9,5},{13... | collective-permute-start | bytes 184328 | tf_op jit(solution)/shard_map/ppermute | solution.py:427
  25.7 2.0 %shard_map.96.inner_ref = f32[2,8,1920]{2,1,0:T(8,128)S(1)} custom-call(s32[4,4,8]{2,1,0:T(4,128)} %bitcast.41, bf16[4,8,6,4,1920]{4,3,2,1,0:T(4,128)(2,1)} %bitcast.35, f32[4,8,1920]{2,1,0:T(8,128)} %bitcast.26), custom_call_target="tpu_custom_call" | custom-call | tf_op jit(solution)/shard_map/pallas_call | solution.py:364
  27.7 0.0 copy-start
  27.8 0.0 copy-start.1
  27.8 0.0 copy-start.2
  27.8 0.0 copy-start.3
  27.8 0.0 copy-start.4
  27.8 8.0 %all-to-all-done.in_ref = f32[16,32,128]{2,1,0:T(8,128)S(1)} async-done(((f32[16,32,128]{2,1,0:T(8,128)}), f32[16,32,128]{2,1,0:T(8,128)S(1)}, u32[]{:S(2)}, u32[]{:S(2)}) %all-to-all-start) | async-done | bytes 262176 | tf_op jit(solution)/shard_map/all_to_all | solution.py:421
  35.8 0.9 shard_map.98
  36.7 6.4 %all-to-all-start.1 = ((f32[16,32,128]{2,1,0:T(8,128)}), f32[16,32,128]{2,1,0:T(8,128)S(1)}, u32[]{:S(2)}, u32[]{:S(2)}) async-start(f32[16,32,128]{2,1,0:T(8,128)} %shard_map.98), calls=%async_computation.1 | async-start | bytes 524288 | tf_op jit(solution)/shard_map/all_to_all | solution.py:421
  43.1 0.0 collective-permute-done.below_ref
  43.1 0.0 collective-permute-done.1.above_ref
  43.2 3.4 %collective-permute-start.3 = (f32[6,1920]{1,0:T(8,128)S(1)}, f32[6,1920]{1,0:T(8,128)S(1)}, u32[]{:S(2)}, u32[]{:S(2)}) collective-permute-start(f32[6,1920]{1,0:T(8,128)S(1)} %pad_maximum_fusion.1), channel_id=1, source_target_pairs={{0,3},{1,0},{2,1},{3,2},{4,7},{5,4},{6,5},{7,6},{8,11},{9,8},{10,9... | collective-permute-start | bytes 138248 | tf_op jit(solution)/shard_map/ppermute | solution.py:432
  46.6 1.9 %collective-permute-start.2 = (f32[6,1920]{1,0:T(8,128)S(1)}, f32[6,1920]{1,0:T(8,128)S(1)}, u32[]{:S(2)}, u32[]{:S(2)}) collective-permute-start(f32[6,1920]{1,0:T(8,128)S(1)} %pad_maximum_fusion), channel_id=1, source_target_pairs={{0,1},{1,2},{2,3},{3,0},{4,5},{5,6},{6,7},{7,4},{8,9},{9,10},{10,1... | collective-permute-start | bytes 138248 | tf_op jit(solution)/shard_map/ppermute | solution.py:431
  48.5 0.0 collective-permute-done.3.right_ref
  48.5 5.1 %collective-permute-done.2.left_ref = f32[6,1920]{1,0:T(8,128)S(1)} collective-permute-done((f32[6,1920]{1,0:T(8,128)S(1)}, f32[6,1920]{1,0:T(8,128)S(1)}, u32[]{:S(2)}, u32[]{:S(2)}) %collective-permute-start.2) | collective-permute-done | bytes 46112 | tf_op jit(solution)/shard_map/ppermute | solution.py:431
  53.6 3.0 %shard_map.97.base_ref = f32[4,8,1920]{2,1,0:T(8,128)S(1)} custom-call(s32[4,4,8]{2,1,0:T(4,128)} %bitcast.42, bf16[4,8,6,4,1920]{4,3,2,1,0:T(4,128)(2,1)} %bitcast.36, f32[4,8,1920]{2,1,0:T(8,128)} %bitcast.27, f32[6,1920]{1,0:T(8,128)S(1)} %collective-permute-done.2.left_ref, f32[6,1920]{1,0:T(8,128)S(1)} %collective-permute-done.3.right_ref, ...), custom_call_target="tpu_custom_call" | custom-call | tf_op jit(solution)/shard_map/pallas_call | solution.py:380
  56.6 3.7 %all-to-all-done.1 = f32[16,32,128]{2,1,0:T(8,128)S(1)} async-done(((f32[16,32,128]{2,1,0:T(8,128)}), f32[16,32,128]{2,1,0:T(8,128)S(1)}, u32[]{:S(2)}, u32[]{:S(2)}) %all-to-all-start.1) | async-done | bytes 262176 | tf_op jit(solution)/shard_map/all_to_all | solution.py:421
  60.3 0.0 copy-done
  60.3 0.0 copy-done.1
  60.3 0.0 copy-done.2
  60.3 0.0 copy-done.3
  60.3 0.0 copy-done.4
  60.4 2.1 %shard_map.99 = (f32[4,8,1920]{2,1,0:T(8,128)S(1)}, f32[512,128]{1,0:T(8,128)}, f32[4,1920]{1,0:T(4,128)S(1)}, f32[4,1920]{1,0:T(4,128)S(1)}) custom-call(f32[4,8,1920]{2,1,0:T(8,128)S(1)} %shard_map.97.base_ref, f32[512,128]{1,0:T(8,128)S(1)} %bitcast.31, f32[4,8,1920]{2,1,0:T(8,128)S(1)} %bitcast.28, bf16[4,6,8,1920]{3,2,1,0:T(8,128)(2,1)S(1)} %bitcast.29, ...), custom_call_target="tpu_custom_call" | custom-call | tf_op jit(solution)/shard_map/pallas_call | solution.py:402
  62.4 8.3 %all-to-all-start.2 = ((f32[16,32,128]{2,1,0:T(8,128)}), f32[16,32,128]{2,1,0:T(8,128)S(1)}, u32[]{:S(2)}, u32[]{:S(2)}) async-start(f32[16,32,128]{2,1,0:T(8,128)} %bitcast.16), calls=%async_computation.2 | async-start | bytes 524288 | tf_op jit(solution)/shard_map/all_to_all | solution.py:421
  70.8 2.6 %collective-permute-start.4 = (f32[8,1920]{1,0:T(8,128)S(1)}, f32[8,1920]{1,0:T(8,128)S(1)}, u32[]{:S(2)}, u32[]{:S(2)}) collective-permute-start(f32[8,1920]{1,0:T(8,128)S(1)} %get-tuple-element.28), channel_id=1, source_target_pairs={{0,4},{4,8},{8,12},{12,16},{16,20},{20,24},{24,28},{1,5},{5,9},{9,... | collective-permute-start | bytes 184328 | tf_op jit(solution)/shard_map/ppermute | solution.py:426
  73.4 2.2 %shard_map.100.inner_ref = f32[2,8,1920]{2,1,0:T(8,128)S(1)} custom-call(s32[4,4,8]{2,1,0:T(4,128)} %bitcast.43, bf16[4,8,6,4,1920]{4,3,2,1,0:T(4,128)(2,1)} %bitcast.37, f32[4,8,1920]{2,1,0:T(8,128)S(1)} %get-tuple-element.20.state_ref), custom_call_target="tpu_custom_call" | custom-call | tf_op jit(solution)/shard_map/pallas_call | solution.py:364
  75.6 4.2 %collective-permute-start.5 = (f32[8,1920]{1,0:T(8,128)S(1)}, f32[8,1920]{1,0:T(8,128)S(1)}, u32[]{:S(2)}, u32[]{:S(2)}) collective-permute-start(f32[8,1920]{1,0:T(8,128)S(1)} %get-tuple-element.29), channel_id=1, source_target_pairs={{4,0},{8,4},{12,8},{16,12},{20,16},{24,20},{28,24},{5,1},{9,5},{13... | collective-permute-start | bytes 184328 | tf_op jit(solution)/shard_map/ppermute | solution.py:427
  79.8 7.6 %all-to-all-done.2.in_ref = f32[16,32,128]{2,1,0:T(8,128)S(1)} async-done(((f32[16,32,128]{2,1,0:T(8,128)}), f32[16,32,128]{2,1,0:T(8,128)S(1)}, u32[]{:S(2)}, u32[]{:S(2)}) %all-to-all-start.2) | async-done | bytes 262176 | tf_op jit(solution)/shard_map/all_to_all | solution.py:421
  87.4 0.9 shard_map.102
  88.2 5.7 %all-to-all-start.3 = ((f32[16,32,128]{2,1,0:T(8,128)}), f32[16,32,128]{2,1,0:T(8,128)S(1)}, u32[]{:S(2)}, u32[]{:S(2)}) async-start(f32[16,32,128]{2,1,0:T(8,128)} %shard_map.102), calls=%async_computation.3 | async-start | bytes 524288 | tf_op jit(solution)/shard_map/all_to_all | solution.py:421
  93.9 0.0 collective-permute-done.4.below_ref
  93.9 0.0 collective-permute-done.5.above_ref
  94.0 1.9 %collective-permute-start.6 = (f32[6,1920]{1,0:T(8,128)S(1)}, f32[6,1920]{1,0:T(8,128)S(1)}, u32[]{:S(2)}, u32[]{:S(2)}) collective-permute-start(f32[6,1920]{1,0:T(8,128)S(1)} %pad_maximum_fusion.2), channel_id=1, source_target_pairs={{0,1},{1,2},{2,3},{3,0},{4,5},{5,6},{6,7},{7,4},{8,9},{9,10},{10,1... | collective-permute-start | bytes 138248 | tf_op jit(solution)/shard_map/ppermute | solution.py:431
  96.0 5.1 %collective-permute-start.7 = (f32[6,1920]{1,0:T(8,128)S(1)}, f32[6,1920]{1,0:T(8,128)S(1)}, u32[]{:S(2)}, u32[]{:S(2)}) collective-permute-start(f32[6,1920]{1,0:T(8,128)S(1)} %pad_maximum_fusion.3), channel_id=1, source_target_pairs={{0,3},{1,0},{2,1},{3,2},{4,7},{5,4},{6,5},{7,6},{8,11},{9,8},{10,9... | collective-permute-start | bytes 138248 | tf_op jit(solution)/shard_map/ppermute | solution.py:432
  101.1 0.0 collective-permute-done.6.left_ref
  101.1 1.8 %collective-permute-done.7.right_ref = f32[6,1920]{1,0:T(8,128)S(1)} collective-permute-done((f32[6,1920]{1,0:T(8,128)S(1)}, f32[6,1920]{1,0:T(8,128)S(1)}, u32[]{:S(2)}, u32[]{:S(2)}) %collective-permute-start.7) | collective-permute-done | bytes 46112 | tf_op jit(solution)/shard_map/ppermute | solution.py:432
  103.0 3.1 %shard_map.101.base_ref = f32[4,8,1920]{2,1,0:T(8,128)S(1)} custom-call(s32[4,4,8]{2,1,0:T(4,128)} %bitcast.44, bf16[4,8,6,4,1920]{4,3,2,1,0:T(4,128)(2,1)} %bitcast.38, f32[4,8,1920]{2,1,0:T(8,128)S(1)} %get-tuple-element.20.state_ref, f32[6,1920]{1,0:T(8,128)S(1)} %collective-permute-done.6.left_ref, f32[6,1920]{1,0:T(8,128)S(1)} %collective-permute-done.7.right_ref, ...), custom_call_target="tpu_custom_call" | custom-call | tf_op jit(solution)/shard_map/pallas_call | solution.py:380
  106.1 4.3 %all-to-all-done.3 = f32[16,32,128]{2,1,0:T(8,128)S(1)} async-done(((f32[16,32,128]{2,1,0:T(8,128)}), f32[16,32,128]{2,1,0:T(8,128)S(1)}, u32[]{:S(2)}, u32[]{:S(2)}) %all-to-all-start.3) | async-done | bytes 262176 | tf_op jit(solution)/shard_map/all_to_all | solution.py:421
  110.4 1.5 %shard_map.103 = (f32[4,8,1920]{2,1,0:T(8,128)}, f32[4,8,1920]{2,1,0:T(8,128)}) custom-call(f32[4,8,1920]{2,1,0:T(8,128)S(1)} %shard_map.101.base_ref, f32[512,128]{1,0:T(8,128)S(1)} %bitcast.32, f32[4,8,1920]{2,1,0:T(8,128)S(1)} %get-tuple-element.20.state_ref, bf16[4,6,8,1920]{3,2,1,0:T(8,128)(2,1)S(1)} %bitcast.30, bf16[72,256]{1,0:T(8,128)(2,1)S(1)} %bitcast.34, ...), custom_call_target="tpu_custom_call" | custom-call | tf_op jit(solution)/shard_map/pallas_call | solution.py:412
  (9 shorter events, 0.2 us)
Async XLA Ops:
  2.8 33.0 %all-to-all-start = ((f32[16,32,128]{2,1,0:T(8,128)}), f32[16,32,128]{2,1,0:T(8,128)S(1)}, u32[]{:S(2)}, u32[]{:S(2)}) async-start(f32[16,32,128]{2,1,0:T(8,128)} %bitcast.8), calls=%async_computation | async-start | bytes 524288 | tf_op jit(solution)/shard_map/all_to_all | solution.py:421
  18.9 24.1 %collective-permute-start = (f32[8,1920]{1,0:T(8,128)S(1)}, f32[8,1920]{1,0:T(8,128)S(1)}, u32[]{:S(2)}, u32[]{:S(2)}) collective-permute-start(f32[8,1920]{1,0:T(8,128)S(1)} %get-tuple-element.30), channel_id=1, source_target_pairs={{0,4},{4,8},{8,12},{12,16},{16,20},{20,24},{24,28},{1,5},{5,9},{9,... | collective-permute-start | bytes 184328 | tf_op jit(solution)/shard_map/ppermute | solution.py:426
  22.4 20.7 %collective-permute-start.1 = (f32[8,1920]{1,0:T(8,128)S(1)}, f32[8,1920]{1,0:T(8,128)S(1)}, u32[]{:S(2)}, u32[]{:S(2)}) collective-permute-start(f32[8,1920]{1,0:T(8,128)S(1)} %get-tuple-element.31), channel_id=1, source_target_pairs={{4,0},{8,4},{12,8},{16,12},{20,16},{24,20},{28,24},{5,1},{9,5},{13... | collective-permute-start | bytes 184328 | tf_op jit(solution)/shard_map/ppermute | solution.py:427
  27.7 32.6 %copy-start = (f32[1,4,8,1920]{3,2,1,0:T(8,128)S(1)}, f32[1,4,8,1920]{3,2,1,0:T(8,128)}, u32[]{:S(2)}) copy-start(f32[1,4,8,1920]{3,2,1,0:T(8,128)} %param.9) | copy-start | bytes 737284
  27.8 32.6 %copy-start.1 = (bf16[1,4,8,6,1920]{4,2,3,1,0:T(8,128)(2,1)S(1)}, bf16[1,4,8,6,1920]{4,2,3,1,0:T(8,128)(2,1)}, u32[]{:S(2)}) copy-start(bf16[1,4,8,6,1920]{4,2,3,1,0:T(8,128)(2,1)} %param.12) | copy-start | bytes 2211844
  27.8 32.6 %copy-start.2 = (bf16[1,72,256]{2,1,0:T(8,128)(2,1)S(1)}, bf16[1,72,256]{2,1,0:T(8,128)(2,1)}, u32[]{:S(2)}) copy-start(bf16[1,72,256]{2,1,0:T(8,128)(2,1)} %param.15) | copy-start | bytes 110596
  27.8 32.6 %copy-start.3 = (s32[2,256]{1,0:T(2,128)S(1)}, s32[2,256]{1,0:T(2,128)}, u32[]{:S(2)}) copy-start(s32[2,256]{1,0:T(2,128)} %src_ref.3) | copy-start | bytes 6148
  27.8 32.6 %copy-start.4 = (s32[2,256]{1,0:T(2,128)S(1)}, s32[2,256]{1,0:T(2,128)}, u32[]{:S(2)}) copy-start(s32[2,256]{1,0:T(2,128)} %dst_ref.3) | copy-start | bytes 6148
  36.7 23.6 %all-to-all-start.1 = ((f32[16,32,128]{2,1,0:T(8,128)}), f32[16,32,128]{2,1,0:T(8,128)S(1)}, u32[]{:S(2)}, u32[]{:S(2)}) async-start(f32[16,32,128]{2,1,0:T(8,128)} %shard_map.98), calls=%async_computation.1 | async-start | bytes 524288 | tf_op jit(solution)/shard_map/all_to_all | solution.py:421
  43.2 5.4 %collective-permute-start.3 = (f32[6,1920]{1,0:T(8,128)S(1)}, f32[6,1920]{1,0:T(8,128)S(1)}, u32[]{:S(2)}, u32[]{:S(2)}) collective-permute-start(f32[6,1920]{1,0:T(8,128)S(1)} %pad_maximum_fusion.1), channel_id=1, source_target_pairs={{0,3},{1,0},{2,1},{3,2},{4,7},{5,4},{6,5},{7,6},{8,11},{9,8},{10,9... | collective-permute-start | bytes 138248 | tf_op jit(solution)/shard_map/ppermute | solution.py:432
  46.6 7.0 %collective-permute-start.2 = (f32[6,1920]{1,0:T(8,128)S(1)}, f32[6,1920]{1,0:T(8,128)S(1)}, u32[]{:S(2)}, u32[]{:S(2)}) collective-permute-start(f32[6,1920]{1,0:T(8,128)S(1)} %pad_maximum_fusion), channel_id=1, source_target_pairs={{0,1},{1,2},{2,3},{3,0},{4,5},{5,6},{6,7},{7,4},{8,9},{9,10},{10,1... | collective-permute-start | bytes 138248 | tf_op jit(solution)/shard_map/ppermute | solution.py:431
  62.4 25.0 %all-to-all-start.2 = ((f32[16,32,128]{2,1,0:T(8,128)}), f32[16,32,128]{2,1,0:T(8,128)S(1)}, u32[]{:S(2)}, u32[]{:S(2)}) async-start(f32[16,32,128]{2,1,0:T(8,128)} %bitcast.16), calls=%async_computation.2 | async-start | bytes 524288 | tf_op jit(solution)/shard_map/all_to_all | solution.py:421
  70.8 23.2 %collective-permute-start.4 = (f32[8,1920]{1,0:T(8,128)S(1)}, f32[8,1920]{1,0:T(8,128)S(1)}, u32[]{:S(2)}, u32[]{:S(2)}) collective-permute-start(f32[8,1920]{1,0:T(8,128)S(1)} %get-tuple-element.28), channel_id=1, source_target_pairs={{0,4},{4,8},{8,12},{12,16},{16,20},{20,24},{24,28},{1,5},{5,9},{9,... | collective-permute-start | bytes 184328 | tf_op jit(solution)/shard_map/ppermute | solution.py:426
  75.6 18.3 %collective-permute-start.5 = (f32[8,1920]{1,0:T(8,128)S(1)}, f32[8,1920]{1,0:T(8,128)S(1)}, u32[]{:S(2)}, u32[]{:S(2)}) collective-permute-start(f32[8,1920]{1,0:T(8,128)S(1)} %get-tuple-element.29), channel_id=1, source_target_pairs={{4,0},{8,4},{12,8},{16,12},{20,16},{24,20},{28,24},{5,1},{9,5},{13... | collective-permute-start | bytes 184328 | tf_op jit(solution)/shard_map/ppermute | solution.py:427
  88.2 22.2 %all-to-all-start.3 = ((f32[16,32,128]{2,1,0:T(8,128)}), f32[16,32,128]{2,1,0:T(8,128)S(1)}, u32[]{:S(2)}, u32[]{:S(2)}) async-start(f32[16,32,128]{2,1,0:T(8,128)} %shard_map.102), calls=%async_computation.3 | async-start | bytes 524288 | tf_op jit(solution)/shard_map/all_to_all | solution.py:421
  94.0 7.1 %collective-permute-start.6 = (f32[6,1920]{1,0:T(8,128)S(1)}, f32[6,1920]{1,0:T(8,128)S(1)}, u32[]{:S(2)}, u32[]{:S(2)}) collective-permute-start(f32[6,1920]{1,0:T(8,128)S(1)} %pad_maximum_fusion.2), channel_id=1, source_target_pairs={{0,1},{1,2},{2,3},{3,0},{4,5},{5,6},{6,7},{7,4},{8,9},{9,10},{10,1... | collective-permute-start | bytes 138248 | tf_op jit(solution)/shard_map/ppermute | solution.py:431
  96.0 7.0 %collective-permute-start.7 = (f32[6,1920]{1,0:T(8,128)S(1)}, f32[6,1920]{1,0:T(8,128)S(1)}, u32[]{:S(2)}, u32[]{:S(2)}) collective-permute-start(f32[6,1920]{1,0:T(8,128)S(1)} %pad_maximum_fusion.3), channel_id=1, source_target_pairs={{0,3},{1,0},{2,1},{3,2},{4,7},{5,4},{6,5},{7,6},{8,11},{9,8},{10,9... | collective-permute-start | bytes 138248 | tf_op jit(solution)/shard_map/ppermute | solution.py:432
